TPU v7x, 32 devices: a whole 2x2x4 slice. The times are simulated.
32 devices in a mesh: dp: 16 (over z, x, core), tensor: 2 (over y).
Axes of the slice: x: 2, y: 2, z: 4, core: 2. Of those that a mesh axis runs over, the one named last changes fastest.
Arguments:
- tokens: bfloat16 [16384, 1024], P(('dp', 'tensor')), may hold values from -6 to 6
- query_weight: bfloat16 [1024, 1024], P('dp', 'tensor'), may hold values from -0.1875 to 0.1875
- key_weight: bfloat16 [1024, 1024], P('dp', 'tensor'), may hold values from -0.1875 to 0.1875
- value_weight: bfloat16 [1024, 1024], P('dp', 'tensor'), may hold values from -0.1875 to 0.1875
- out_weight: bfloat16 [1024, 1024], P('tensor', 'dp'), may hold values from -0.1875 to 0.1875
- gate_weight: bfloat16 [1024, 2816], P('dp', 'tensor'), may hold values from -0.1875 to 0.1875
- up_weight: bfloat16 [1024, 2816], P('dp', 'tensor'), may hold values from -0.1875 to 0.1875
- down_weight: bfloat16 [2816, 1024], P('tensor', 'dp'), may hold values from -0.109375 to 0.109375
- gain_attn_in: bfloat16 [1024], P('dp'), may hold values from 0.5 to 1.5
- gain_attn_out: bfloat16 [1024], P('dp'), may hold values from 0.5 to 1.5
- gain_ff_in: bfloat16 [1024], P('dp'), may hold values from 0.5 to 1.5
- gain_ff_out: bfloat16 [1024], P('dp'), may hold values from 0.5 to 1.5
- piece_starts: int32 [16, 2], P('dp'), may hold values from 0 to 768, as said below
- out_grad: bfloat16 [16384, 1024], P(('dp', 'tensor')), may hold values from -6 to 6
Outputs:
- layer_out: bfloat16 [16384, 1024], P(('dp', 'tensor'))
- input_grad: float32 [16384, 1024], P(('dp', 'tensor'))
- grad_query: float32 [1024, 1024], P('dp', 'tensor')
- grad_key: float32 [1024, 1024], P('dp', 'tensor')
- grad_value: float32 [1024, 1024], P('dp', 'tensor')
- grad_out: float32 [1024, 1024], P('tensor', 'dp')
- grad_gate: float32 [1024, 2816], P('dp', 'tensor')
- grad_up: float32 [1024, 2816], P('dp', 'tensor')
- grad_down: float32 [2816, 1024], P('tensor', 'dp')
- grad_gain_attn_in: float32 [1024], P('dp')
- grad_gain_attn_out: float32 [1024], P('dp')
- grad_gain_ff_in: float32 [1024], P('dp')
- grad_gain_ff_out: float32 [1024], P('dp')
Inputs may be any that keep to these rules, and one draw needn't show every extreme that they name: `piece_starts`: each sequence's 2 pieces of 256 tokens are disjoint and in order: piece number k starts between k * 512 and (k + 1) * 512 - 256. In the first sequence the first piece starts at 0 and the last piece ends at the sequence's end.
All inputs are finite; a program needn't handle non-finite values.
Results may differ from a plain program's by a relative error of at most 0.023.
Values may be sent and summed in bfloat16 or wider, within the bound.
A program may use at most 192 MiB of HBM per device.

v0:
```python
import math

import jax
import jax.numpy as jnp
from jax import lax
from jax.sharding import PartitionSpec as P

HEAD_DIM = 128
PIECE = 256


norm_eps = 1e-06
rope_base = 50000.0
masked = -1e30


def rms_scale(values):
    return lax.rsqrt(jnp.mean(values * values, axis=-1, keepdims=True) + norm_eps)


def norm_back(values, scale, gain, incoming):
    weighted = gain * incoming
    row_inner = jnp.mean(values * weighted, axis=-1, keepdims=True)
    backward = scale * weighted - values * (scale * scale * scale) * row_inner
    return (backward, jnp.sum(values * scale * incoming, axis=0))


def rope_at(places):
    half_dim = HEAD_DIM // 2
    inverse = rope_base ** (-(jnp.arange(half_dim, dtype=jnp.float32) * 2.0) / HEAD_DIM)
    angles = places.astype(jnp.float32)[:, None, None] * inverse[None, None, :]
    return (jnp.cos(angles), jnp.sin(angles))


def rope_tables(count, length):
    return rope_at(jnp.arange(count, dtype=jnp.int32) % length)


def rotate(values, cosine, sine):
    half_dim = values.shape[-1] // 2
    lower_half = values[..., :half_dim]
    upper_half = values[..., half_dim:]
    return jnp.concatenate(
        [lower_half * cosine - upper_half * sine, upper_half * cosine + lower_half * sine], axis=-1
    )


def unrotate(grads, cosine, sine):
    half_dim = grads.shape[-1] // 2
    lower_half = grads[..., :half_dim]
    upper_half = grads[..., half_dim:]
    return jnp.concatenate(
        [lower_half * cosine + upper_half * sine, upper_half * cosine - lower_half * sine], axis=-1
    )


def piece_ids(starts, length):
    places = jnp.arange(length, dtype=jnp.int32)
    inside = (places[None, :, None] >= starts[:, None, :]) & (
        places[None, :, None] < starts[:, None, :] + PIECE
    )
    labels = jnp.arange(1, starts.shape[1] + 1, dtype=jnp.int32)
    return jnp.sum(jnp.where(inside, labels, 0), axis=2)


def visible(piece_id, offset, count):
    length = piece_id.shape[0]
    query_place = offset + jnp.arange(count, dtype=jnp.int32)
    key_place = jnp.arange(length, dtype=jnp.int32)
    query_ids = piece_id[offset : offset + count]
    return (key_place[None, :] <= query_place[:, None]) | (
        query_ids[:, None] == piece_id[None, :]
    ) & (query_ids[:, None] > 0)


def block_scores(queries, key_vecs, piece_id, offset, count):
    attn_scale = 1.0 / math.sqrt(queries.shape[-1])
    q_block = queries[offset : offset + count]
    scores = (
        jnp.einsum("qhd,khd->hqk", q_block, key_vecs, preferred_element_type=jnp.float32)
        * attn_scale
    )
    return (jnp.where(visible(piece_id, offset, count)[None], scores, masked), q_block)


def attend_one(seq_items):
    queries, key_vecs, values, piece_id = seq_items
    length = queries.shape[0]
    block_rows = min(512, length)
    outputs = []
    log_totals = []
    for offset in range(0, length, block_rows):
        logits, q_block = block_scores(queries, key_vecs, piece_id, offset, block_rows)
        row_max = jnp.max(logits, axis=-1, keepdims=True)
        log_total = row_max + jnp.log(jnp.sum(jnp.exp(logits - row_max), axis=-1, keepdims=True))
        probs = jnp.exp(logits - log_total).astype(jnp.bfloat16)
        mixed = jnp.einsum("hqk,khd->qhd", probs, values, preferred_element_type=jnp.float32)
        outputs.append(mixed.astype(jnp.bfloat16))
        log_totals.append(log_total)
    return (jnp.concatenate(outputs, axis=0), jnp.concatenate(log_totals, axis=1))


def attend_back(seq_items):
    queries, key_vecs, values, piece_id, log_totals, grad_mixed = seq_items
    length = queries.shape[0]
    block_rows = min(512, length)
    attn_scale = 1.0 / math.sqrt(queries.shape[-1])
    grad_keys = jnp.zeros(key_vecs.shape, jnp.float32)
    grad_values = jnp.zeros(values.shape, jnp.float32)
    grad_queries = []
    for offset in range(0, length, block_rows):
        logits, q_block = block_scores(queries, key_vecs, piece_id, offset, block_rows)
        probs = jnp.exp(logits - log_totals[:, offset : offset + block_rows])
        grad_block = grad_mixed[offset : offset + block_rows]
        grad_values = grad_values + jnp.einsum(
            "hqk,qhd->khd",
            probs.astype(jnp.bfloat16),
            grad_block,
            preferred_element_type=jnp.float32,
        )
        grad_probs = jnp.einsum(
            "qhd,khd->hqk", grad_block, values, preferred_element_type=jnp.float32
        )
        row_inner = jnp.sum(probs * grad_probs, axis=-1, keepdims=True)
        grad_scores = (probs * (grad_probs - row_inner) * attn_scale).astype(jnp.bfloat16)
        grad_queries.append(
            jnp.einsum("hqk,khd->qhd", grad_scores, key_vecs, preferred_element_type=jnp.float32)
        )
        grad_keys = grad_keys + jnp.einsum(
            "hqk,qhd->khd", grad_scores, q_block, preferred_element_type=jnp.float32
        )
    return (jnp.concatenate(grad_queries, axis=0), grad_keys, grad_values)


def times_trans(left, right):
    return lax.dot_general(
        left, right, (((1,), (1,)), ((), ())), preferred_element_type=jnp.float32
    )


def trans_times(left, right):
    return lax.dot_general(
        left, right, (((0,), (0,)), ((), ())), preferred_element_type=jnp.float32
    )


def fetch_weights(shards):
    gathered = (
        lax.all_gather(shards[0], "dp", axis=0, tiled=True),
        lax.all_gather(shards[1], "dp", axis=0, tiled=True),
        lax.all_gather(shards[2], "dp", axis=0, tiled=True),
        lax.all_gather(shards[3], "dp", axis=1, tiled=True),
        lax.all_gather(shards[4], "dp", axis=0, tiled=True),
        lax.all_gather(shards[5], "dp", axis=0, tiled=True),
        lax.all_gather(shards[6], "dp", axis=1, tiled=True),
        lax.all_gather(shards[7], "dp", axis=1, tiled=True),
    )
    return gathered


def gather_rows(normed):
    return lax.all_gather(normed, "tensor", axis=0, tiled=True)


def sum_rows(sum_terms):
    return lax.psum_scatter(sum_terms, "tensor", scatter_dimension=0, tiled=True)


def gather_grads(grad_terms):
    return lax.all_gather(grad_terms, "tensor", axis=0, tiled=True)


def sum_grads(grad_terms):
    return lax.psum_scatter(
        grad_terms.astype(jnp.bfloat16), "tensor", scatter_dimension=0, tiled=True
    ).astype(jnp.float32)


def by_sequence(values, seq_count):
    return values.reshape(seq_count, values.shape[0] // seq_count, values.shape[1], values.shape[2])


def attention_part(normed, gathered, cosine, sine, piece_id):
    whole_rows = gather_rows(normed)
    group_rows = whole_rows.shape[0]
    seq_count = piece_id.shape[0]

    def project(weight):
        return jnp.dot(whole_rows, weight, preferred_element_type=jnp.float32).reshape(
            group_rows, -1, HEAD_DIM
        )

    queries = rotate(project(gathered[0]), cosine, sine).astype(jnp.bfloat16)
    key_vecs = rotate(project(gathered[1]), cosine, sine).astype(jnp.bfloat16)
    values = project(gathered[2]).astype(jnp.bfloat16)
    outputs, log_totals = lax.map(
        attend_one,
        (
            by_sequence(queries, seq_count),
            by_sequence(key_vecs, seq_count),
            by_sequence(values, seq_count),
            piece_id,
        ),
    )
    return (whole_rows, queries, key_vecs, values, outputs.reshape(group_rows, -1), log_totals)


def feed_part(normed, gathered):
    whole_rows = gather_rows(normed)
    gate_pre = jnp.dot(whole_rows, gathered[4], preferred_element_type=jnp.float32)
    up_pre = jnp.dot(whole_rows, gathered[5], preferred_element_type=jnp.float32)
    hidden = (jax.nn.silu(gate_pre) * up_pre).astype(jnp.bfloat16)
    return (whole_rows, gate_pre, up_pre, hidden)


def on_device(
    tokens,
    query_weight,
    key_weight,
    value_weight,
    out_weight,
    gate_weight,
    up_weight,
    down_weight,
    gain_attn_in,
    gain_attn_out,
    gain_ff_in,
    gain_ff_out,
    piece_starts,
    out_grad,
):
    shards = (
        query_weight,
        key_weight,
        value_weight,
        out_weight,
        gate_weight,
        up_weight,
        down_weight,
        jnp.stack([gain_attn_in, gain_attn_out, gain_ff_in, gain_ff_out]),
    )
    gathered = fetch_weights(shards)
    gain_rows = gathered[7].astype(jnp.float32)
    tok_rows = tokens.astype(jnp.float32)
    seq_count = piece_starts.shape[0]
    own_rows = tokens.shape[0]
    group_rows = own_rows * lax.axis_size("tensor")
    length = group_rows // seq_count
    piece_id = piece_ids(piece_starts, length)
    incoming = out_grad.astype(jnp.float32)
    scale_in = rms_scale(tok_rows)
    normed_in = (tok_rows * scale_in * gain_rows[0]).astype(jnp.bfloat16)
    cosine, sine = rope_tables(group_rows, length)
    attn_parts = attention_part(normed_in, gathered, cosine, sine, piece_id)
    branch_attn = sum_rows(jnp.dot(attn_parts[4], gathered[3], preferred_element_type=jnp.float32))
    scale_attn = rms_scale(branch_attn)
    mid_rows = tok_rows + branch_attn * scale_attn * gain_rows[1]
    scale_mid = rms_scale(mid_rows)
    normed_ff = (mid_rows * scale_mid * gain_rows[2]).astype(jnp.bfloat16)
    feed_parts = feed_part(normed_ff, gathered)
    branch_ff = sum_rows(jnp.dot(feed_parts[3], gathered[6], preferred_element_type=jnp.float32))
    scale_ff = rms_scale(branch_ff)
    result = (mid_rows + branch_ff * scale_ff * gain_rows[3]).astype(jnp.bfloat16)
    gathered = fetch_weights(shards)
    feed_parts = feed_part(normed_ff, gathered)
    whole_ff, gate_pre, up_pre, hidden = feed_parts
    back_ff, gain_grad_ff_out = norm_back(branch_ff, scale_ff, gain_rows[3], incoming)
    wide_back_ff = gather_grads(back_ff.astype(jnp.bfloat16))
    grad_down = trans_times(hidden, wide_back_ff)
    back_hidden = times_trans(wide_back_ff, gathered[6])
    sigmoid_gate = jax.nn.sigmoid(gate_pre)
    back_gate = (
        back_hidden * up_pre * sigmoid_gate * (1.0 + gate_pre * (1.0 - sigmoid_gate))
    ).astype(jnp.bfloat16)
    back_up = (back_hidden * gate_pre * sigmoid_gate).astype(jnp.bfloat16)
    grad_gate = trans_times(whole_ff, back_gate)
    grad_up = trans_times(whole_ff, back_up)
    back_normed_ff = sum_grads(
        times_trans(back_gate, gathered[4]) + times_trans(back_up, gathered[5])
    )
    back_from_ff, gain_grad_ff_in = norm_back(mid_rows, scale_mid, gain_rows[2], back_normed_ff)
    back_mid = incoming + back_from_ff
    back_attn, gain_grad_attn_out = norm_back(branch_attn, scale_attn, gain_rows[1], back_mid)
    wide_back_attn = gather_grads(back_attn.astype(jnp.bfloat16))
    attn_parts = attention_part(normed_in, gathered, cosine, sine, piece_id)
    whole_in, queries, key_vecs, values, attended, log_totals = attn_parts
    grad_out = trans_times(attended, wide_back_attn)
    back_attended = times_trans(wide_back_attn, gathered[3]).astype(jnp.bfloat16)
    back_queries, back_keys, back_values = lax.map(
        attend_back,
        (
            by_sequence(queries, seq_count),
            by_sequence(key_vecs, seq_count),
            by_sequence(values, seq_count),
            piece_id,
            log_totals,
            by_sequence(back_attended.reshape(group_rows, -1, HEAD_DIM), seq_count),
        ),
    )
    back_queries = (
        unrotate(back_queries.reshape(group_rows, -1, HEAD_DIM), cosine, sine)
        .reshape(group_rows, -1)
        .astype(jnp.bfloat16)
    )
    back_keys = (
        unrotate(back_keys.reshape(group_rows, -1, HEAD_DIM), cosine, sine)
        .reshape(group_rows, -1)
        .astype(jnp.bfloat16)
    )
    back_values = back_values.reshape(group_rows, -1).astype(jnp.bfloat16)
    grad_query = trans_times(whole_in, back_queries)
    grad_key = trans_times(whole_in, back_keys)
    grad_value = trans_times(whole_in, back_values)
    back_normed_in = sum_grads(
        times_trans(back_queries, gathered[0])
        + times_trans(back_keys, gathered[1])
        + times_trans(back_values, gathered[2])
    )
    back_from_in, gain_grad_attn_in = norm_back(tok_rows, scale_in, gain_rows[0], back_normed_in)
    input_grad = back_mid + back_from_in
    weight_terms = (grad_query, grad_key, grad_value, grad_out, grad_gate, grad_up, grad_down)
    gain_grads = lax.psum(
        jnp.stack([gain_grad_attn_in, gain_grad_attn_out, gain_grad_ff_in, gain_grad_ff_out]),
        "tensor",
    )
    grad_sums = (
        lax.psum_scatter(
            weight_terms[0].astype(jnp.bfloat16), "dp", scatter_dimension=0, tiled=True
        ).astype(jnp.float32),
        lax.psum_scatter(
            weight_terms[1].astype(jnp.bfloat16), "dp", scatter_dimension=0, tiled=True
        ).astype(jnp.float32),
        lax.psum_scatter(
            weight_terms[2].astype(jnp.bfloat16), "dp", scatter_dimension=0, tiled=True
        ).astype(jnp.float32),
        lax.psum_scatter(
            weight_terms[3].astype(jnp.bfloat16), "dp", scatter_dimension=1, tiled=True
        ).astype(jnp.float32),
        lax.psum_scatter(
            weight_terms[4].astype(jnp.bfloat16), "dp", scatter_dimension=0, tiled=True
        ).astype(jnp.float32),
        lax.psum_scatter(
            weight_terms[5].astype(jnp.bfloat16), "dp", scatter_dimension=0, tiled=True
        ).astype(jnp.float32),
        lax.psum_scatter(
            weight_terms[6].astype(jnp.bfloat16), "dp", scatter_dimension=1, tiled=True
        ).astype(jnp.float32),
        lax.psum_scatter(
            gain_grads.astype(jnp.bfloat16), "dp", scatter_dimension=1, tiled=True
        ).astype(jnp.float32),
    )
    return (
        result,
        input_grad,
        grad_sums[0],
        grad_sums[1],
        grad_sums[2],
        grad_sums[3],
        grad_sums[4],
        grad_sums[5],
        grad_sums[6],
        grad_sums[7][0],
        grad_sums[7][1],
        grad_sums[7][2],
        grad_sums[7][3],
    )


def solution(mesh):
    placed = (
        P(("dp", "tensor"), None),
        P("dp", "tensor"),
        P("dp", "tensor"),
        P("dp", "tensor"),
        P("tensor", "dp"),
        P("dp", "tensor"),
        P("dp", "tensor"),
        P("tensor", "dp"),
        P("dp"),
        P("dp"),
        P("dp"),
        P("dp"),
        P("dp", None),
        P(("dp", "tensor"), None),
    )
    return jax.shard_map(
        on_device,
        mesh=mesh,
        in_specs=placed,
        out_specs=(
            P(("dp", "tensor"), None),
            P(("dp", "tensor"), None),
            P("dp", "tensor"),
            P("dp", "tensor"),
            P("dp", "tensor"),
            P("tensor", "dp"),
            P("dp", "tensor"),
            P("dp", "tensor"),
            P("tensor", "dp"),
            P("dp"),
            P("dp"),
            P("dp"),
            P("dp"),
        ),
        check_vma=False,
    )
```

profile of v0, /device:TPU:0, one launch (start us, length us, event | category | flops | bytes accessed | tf_op | source)
XLA Modules:
  0.0 1177.9 jit_solution(7611702751762678981)
XLA Ops:
  8.7 23.1 %all-gather = bf16[16,64,4]{1,2,0:T(4,128)(2,1)S(1)} all-gather(bf16[1,64,4]{1,2,0:T(4,128)(2,1)S(1)} %maximum_bitcast_fusion), channel_id=1, replica_groups=mesh['dp'=16,'tensor'=2] {'dp'}, dimensions={0}, use_global_device_ids=true | all-gather | bytes 8704 | tf_op jit(solution)/shard_map/all_gather | solution.py:156
  43.1 7.7 all-gather.19.cloned.1.call-done
  50.9 34.2 %all-gather.13.cloned.1.call-done = bf16[1024,1024]{1,0:T(8,128)(2,1)} async-done(((bf16[512,1024]{1,0:T(8,128)(2,1)}), bf16[1024,1024]{1,0:T(8,128)(2,1)}) %all-gather.13.cloned.1.call-update) | async-done | bytes 2097168 | tf_op jit(solution)/shard_map/all_gather | solution.py:162
  94.7 30.5 %all-gather.17.cloned.1.call-done = bf16[1024,512]{1,0:T(8,128)(2,1)} async-done(((bf16[64,512]{1,0:T(8,128)(2,1)}), bf16[1024,512]{1,0:T(8,128)(2,1)}) %all-gather.17.cloned.1.call-update) | async-done | bytes 1048592 | tf_op jit(solution)/shard_map/all_gather | solution.py:149
  152.2 11.9 %all-gather.15.cloned.1.call-done = bf16[1024,512]{1,0:T(8,128)(2,1)} async-done(((bf16[64,512]{1,0:T(8,128)(2,1)}), bf16[1024,512]{1,0:T(8,128)(2,1)}) %all-gather.15.cloned.1.call-update) | async-done | bytes 1048592 | tf_op jit(solution)/shard_map/all_gather | solution.py:151
  175.7 27.3 %all-gather.21.cloned.1.call-done = bf16[512,1024]{0,1:T(8,128)(2,1)} async-done(((bf16[512,64]{0,1:T(8,128)(2,1)}), bf16[512,1024]{0,1:T(8,128)(2,1)}) %all-gather.21.cloned.1.call-update) | async-done | bytes 1048592 | tf_op jit(solution)/shard_map/all_gather | solution.py:152
  208.3 52.6 %reduce-scatter.15.cloned.1.call-done = f32[512,1024]{1,0:T(8,128)} async-done(((f32[1024,1024]{1,0:T(8,128)}), f32[512,1024]{1,0:T(8,128)}) %reduce-scatter.15.cloned.1.call-update) | async-done | bytes 2097168 | tf_op jit(solution)/shard_map/reduce_scatter | solution.py:166
  266.8 41.1 %all-gather.25.cloned.1.call-done = bf16[1024,1408]{1,0:T(8,128)(2,1)} async-done(((bf16[64,1408]{1,0:T(8,128)(2,1)}), bf16[1024,1408]{1,0:T(8,128)(2,1)}) %all-gather.25.cloned.1.call-update) | async-done | bytes 2883600 | tf_op jit(solution)/shard_map/all_gather | solution.py:153
  307.9 33.7 %all-gather.23.cloned.1.call-done = bf16[1024,1024]{1,0:T(8,128)(2,1)} async-done(((bf16[512,1024]{1,0:T(8,128)(2,1)}), bf16[1024,1024]{1,0:T(8,128)(2,1)}) %all-gather.23.cloned.1.call-update) | async-done | bytes 2097168 | tf_op jit(solution)/shard_map/all_gather | solution.py:162
  341.5 8.4 fusion.130
  349.9 38.6 %all-gather.27.cloned.1.call-done = bf16[1024,1408]{1,0:T(8,128)(2,1)} async-done(((bf16[64,1408]{1,0:T(8,128)(2,1)}), bf16[1024,1408]{1,0:T(8,128)(2,1)}) %all-gather.27.cloned.1.call-update) | async-done | bytes 2883600 | tf_op jit(solution)/shard_map/all_gather | solution.py:154
  388.5 11.1 multiply_convert_fusion.4
  399.6 34.0 %all-gather.29.cloned.1.call-done = bf16[1408,1024]{0,1:T(8,128)(2,1)} async-done(((bf16[1408,64]{0,1:T(8,128)(2,1)}), bf16[1408,1024]{0,1:T(8,128)(2,1)}) %all-gather.29.cloned.1.call-update) | async-done | bytes 2883600 | tf_op jit(solution)/shard_map/all_gather | solution.py:155
  433.6 8.1 fusion.131
  441.7 52.7 %reduce-scatter.17.cloned.1.call-done = f32[512,1024]{1,0:T(8,128)} async-done(((f32[1024,1024]{1,0:T(8,128)}), f32[512,1024]{1,0:T(8,128)}) %reduce-scatter.17.cloned.1.call-update) | async-done | bytes 2097168 | tf_op jit(solution)/shard_map/reduce_scatter | solution.py:166
  499.7 33.0 %all-gather.31.cloned.1.call-done = bf16[1024,1024]{1,0:T(8,128)(2,1)} async-done(((bf16[512,1024]{1,0:T(8,128)(2,1)}), bf16[1024,1024]{1,0:T(8,128)(2,1)}) %all-gather.31.cloned.1.call-update) | async-done | bytes 2097168 | tf_op jit(solution)/shard_map/all_gather | solution.py:170
  532.8 10.6 multiply_convert_fusion.2
  552.0 32.0 %reduce-scatter.19.cloned.1.call-done = bf16[512,1024]{1,0:T(8,128)(2,1)} async-done(((bf16[1024,1024]{1,0:T(8,128)(2,1)}), bf16[512,1024]{1,0:T(8,128)(2,1)}) %reduce-scatter.19.cloned.1.call-update) | async-done | bytes 1048592 | tf_op jit(solution)/shard_map/reduce_scatter | solution.py:174
  613.4 10.4 all-gather.33.cloned.1.call-done
  632.9 23.2 %fusion.83 = f32[512,4,128]{2,0,1:T(8,128)} fusion(bf16[1024,4,128]{2,0,1:T(8,128)(2,1)S(1)} %copy-done.10, f32[4,512,1024]{2,1,0:T(8,128)} %fusion.133, f32[4,512,1024]{2,1,0:T(8,128)} %copy-done.1, f32[4,512]{1,0:T(4,128)S(1)} %log_add_fusion.1, pred[512,1024]{1,0:T(8,128)(4,1)} %copy-done.18), kind=kOutput, calls=%fused_computation.110 | convolution fusion | flops 559942656 | bytes 19406848 | tf_op jit(solution)/shard_map/while/body/eval_jaxpr/hqk,khd->qhd/dot_general | solution.py:127
  656.1 26.6 %fusion.12 = f32[4,128,1024]{1,2,0:T(8,128)} fusion(f32[4,512,1024]{2,1,0:T(8,128)} %fusion.133, f32[4,512,1024]{2,1,0:T(8,128)} %copy-done.1, f32[4,512]{1,0:T(4,128)S(1)} %log_add_fusion.1, pred[512,1024]{1,0:T(8,128)(4,1)} %copy-done.18, bf16[1024,4,64]{2,0,1:T(8,128)(2,1)S(1)} %copy-done.15, bf16[1024,4,64]{2,0,1:T(8,128)(2,1)S(1)} %copy-done.13), kind=kOutput, calls=%fused_computation.21 | convolution fusion | flops 560991232 | bytes 38813696 | tf_op jit(solution)/shard_map/while/body/eval_jaxpr/hqk,qhd->khd/dot_general | solution.py:129
  687.0 7.3 fusion.116
  709.2 19.1 %fusion.80 = f32[512,4,128]{2,0,1:T(8,128)} fusion(bf16[1024,4,128]{2,0,1:T(8,128)(2,1)S(1)} %copy-done.10, f32[4,512,1024]{2,1,0:T(8,128)} %fusion.134, f32[4,512,1024]{2,1,0:T(8,128)} %copy-done, f32[4,512]{1,0:T(4,128)S(1)} %log_add_fusion, pred[512,1024]{1,0:T(8,128)(4,1)S(1)} %copy-done.17), kind=kOutput, calls=%fused_computation.109 | convolution fusion | flops 559942656 | bytes 19406848 | tf_op jit(solution)/shard_map/while/body/eval_jaxpr/hqk,khd->qhd/dot_general | solution.py:127
  728.3 21.3 %add_bitcast_fusion = f32[1024,4,128]{2,0,1:T(8,128)S(1)} fusion(f32[4,128,1024]{1,2,0:T(8,128)} %fusion.12, bf16[512,4,128]{2,0,1:T(8,128)(2,1)} %copy-done.27, f32[4,512,1024]{2,1,0:T(8,128)} %fusion.134, f32[4,512,1024]{2,1,0:T(8,128)} %copy-done, f32[4,512]{1,0:T(4,128)S(1)} %log_add_fusion, pred[512,1024]{1,0:T(8,128)(4,1)S(1)} %copy-done.17), kind=kOutput, calls=%fused_computation.85 | convolution fusion | flops 560466944 | bytes 22028288 | tf_op jit(solution)/shard_map/while/body/eval_jaxpr/hqk,qhd->khd/dot_general | solution.py:129
  777.6 51.5 %reduce-scatter.31.cloned.1.call-done = bf16[64,1408]{1,0:T(8,128)(2,1)} async-done(((bf16[1024,1408]{1,0:T(8,128)(2,1)}), bf16[64,1408]{1,0:T(8,128)(2,1)}) %reduce-scatter.31.cloned.1.call-update) | async-done | bytes 180240 | tf_op jit(solution)/shard_map/reduce_scatter | solution.py:339
  830.7 58.2 %reduce-scatter.29.cloned.1.call-done = bf16[512,64]{0,1:T(8,128)(2,1)} async-done(((bf16[512,1024]{0,1:T(8,128)(2,1)}), bf16[512,64]{0,1:T(8,128)(2,1)}) %reduce-scatter.29.cloned.1.call-update) | async-done | bytes 65552 | tf_op jit(solution)/shard_map/reduce_scatter | solution.py:336
  890.4 59.0 %reduce-scatter.27.cloned.1.call-done = bf16[64,512]{1,0:T(8,128)(2,1)} async-done(((bf16[1024,512]{1,0:T(8,128)(2,1)}), bf16[64,512]{1,0:T(8,128)(2,1)}) %reduce-scatter.27.cloned.1.call-update) | async-done | bytes 65552 | tf_op jit(solution)/shard_map/reduce_scatter | solution.py:333
  950.9 58.4 %reduce-scatter.25.cloned.1.call-done = bf16[64,512]{1,0:T(8,128)(2,1)} async-done(((bf16[1024,512]{1,0:T(8,128)(2,1)}), bf16[64,512]{1,0:T(8,128)(2,1)}) %reduce-scatter.25.cloned.1.call-update) | async-done | bytes 65552 | tf_op jit(solution)/shard_map/reduce_scatter | solution.py:330
  1010.8 59.0 %reduce-scatter.23.cloned.1.call-done = bf16[64,512]{1,0:T(8,128)(2,1)} async-done(((bf16[1024,512]{1,0:T(8,128)(2,1)}), bf16[64,512]{1,0:T(8,128)(2,1)}) %reduce-scatter.23.cloned.1.call-update) | async-done | bytes 65552 | tf_op jit(solution)/shard_map/reduce_scatter | solution.py:327
  1071.3 31.6 %reduce-scatter.21.cloned.1.call-done = bf16[512,1024]{1,0:T(8,128)(2,1)} async-done(((bf16[1024,1024]{1,0:T(8,128)(2,1)}), bf16[512,1024]{1,0:T(8,128)(2,1)}) %reduce-scatter.21.cloned.1.call-update) | async-done | bytes 1048592 | tf_op jit(solution)/shard_map/reduce_scatter | solution.py:174
  1105.1 7.0 psum.7
  1116.2 53.4 %reduce-scatter.37.cloned.1.call-done = bf16[64,4]{1,0:T(8,128)(2,1)} async-done(((bf16[1024,4]{1,0:T(8,128)(2,1)}), bf16[64,4]{1,0:T(8,128)(2,1)}) %reduce-scatter.37.cloned.1.call-update) | async-done | bytes 528
  (248 shorter events, 186.3 us)
Async XLA Ops:
  7.2 43.7 %all-gather.19.cloned.1.call-start = ((), (), s32[]{:S(2)}) async-start(), calls=%async_computation.15 | async-start | bytes 1114112 | tf_op jit(solution)/shard_map/all_gather | solution.py:150
  7.9 77.1 %all-gather.13.cloned.1.call-start = ((), (), s32[]{:S(2)}) async-start(), calls=%async_computation.12 | async-start | bytes 3145728 | tf_op jit(solution)/shard_map/all_gather | solution.py:162
  36.5 88.7 %all-gather.17.cloned.1.call-start = ((), (), s32[]{:S(2)}) async-start(), calls=%async_computation.14 | async-start | bytes 1114112 | tf_op jit(solution)/shard_map/all_gather | solution.py:149
  37.2 126.9 %all-gather.15.cloned.1.call-start = ((), (), s32[]{:S(2)}) async-start(), calls=%async_computation.13 | async-start | bytes 1114112 | tf_op jit(solution)/shard_map/all_gather | solution.py:151
  37.8 165.2 %all-gather.21.cloned.1.call-start = ((), (), s32[]{:S(2)}) async-start(), calls=%async_computation.16 | async-start | bytes 1114112 | tf_op jit(solution)/shard_map/all_gather | solution.py:152
  38.4 222.5 %reduce-scatter.15.cloned.1.call-start = ((), (), s32[]{:S(2)}) async-start(), calls=%async_computation.17 | async-start | bytes 6291456 | tf_op jit(solution)/shard_map/reduce_scatter | solution.py:166
  43.1 123.7 %copy-start.16 = (pred[512,1024]{1,0:T(8,128)(4,1)}, pred[512,1024]{1,0:T(8,128)(4,1)S(1)}, u32[]{:S(2)}) copy-start(pred[512,1024]{1,0:T(8,128)(4,1)S(1)} %get-tuple-element.122) | copy-start | bytes 1572868
  43.1 129.9 %copy-start.18 = (pred[512,1024]{1,0:T(8,128)(4,1)}, pred[512,1024]{1,0:T(8,128)(4,1)S(1)}, u32[]{:S(2)}) copy-start(pred[512,1024]{1,0:T(8,128)(4,1)S(1)} %get-tuple-element.121) | copy-start | bytes 1572868
  207.5 55.4 %copy-start.4 = (bf16[512,1024]{1,0:T(8,128)(2,1)S(1)}, bf16[512,1024]{1,0:T(8,128)(2,1)}, u32[]{:S(2)}) copy-start(bf16[512,1024]{1,0:T(8,128)(2,1)} %param.14) | copy-start | bytes 3145732
  207.5 100.3 %all-gather.25.cloned.1.call-start = ((), (), s32[]{:S(2)}) async-start(), calls=%async_computation.19 | async-start | bytes 3063808 | tf_op jit(solution)/shard_map/all_gather | solution.py:153
  208.3 133.2 %all-gather.23.cloned.1.call-start = ((), (), s32[]{:S(2)}) async-start(), calls=%async_computation.18 | async-start | bytes 3145728 | tf_op jit(solution)/shard_map/all_gather | solution.py:162
  265.0 123.5 %all-gather.27.cloned.1.call-start = ((), (), s32[]{:S(2)}) async-start(), calls=%async_computation.20 | async-start | bytes 3063808 | tf_op jit(solution)/shard_map/all_gather | solution.py:154
  265.8 167.8 %all-gather.29.cloned.1.call-start = ((), (), s32[]{:S(2)}) async-start(), calls=%async_computation.21 | async-start | bytes 3063808 | tf_op jit(solution)/shard_map/all_gather | solution.py:155
  266.3 228.1 %reduce-scatter.17.cloned.1.call-start = ((), (), s32[]{:S(2)}) async-start(), calls=%async_computation.22 | async-start | bytes 6291456 | tf_op jit(solution)/shard_map/reduce_scatter | solution.py:166
  441.7 54.8 %copy-start.11 = (bf16[512,1024]{1,0:T(8,128)(2,1)S(1)}, bf16[512,1024]{1,0:T(8,128)(2,1)}, u32[]{:S(2)}) copy-start(bf16[512,1024]{1,0:T(8,128)(2,1)} %param.27) | copy-start | bytes 3145732
  441.7 91.1 %all-gather.31.cloned.1.call-start = ((), (), s32[]{:S(2)}) async-start(), calls=%async_computation.23 | async-start | bytes 3145728 | tf_op jit(solution)/shard_map/all_gather | solution.py:170
  499.5 84.5 %reduce-scatter.19.cloned.1.call-start = ((), (), s32[]{:S(2)}) async-start(), calls=%async_computation.24 | async-start | bytes 3145728 | tf_op jit(solution)/shard_map/reduce_scatter | solution.py:174
  552.0 71.8 %all-gather.33.cloned.1.call-start = ((), (), s32[]{:S(2)}) async-start(), calls=%async_computation.25 | async-start | bytes 3145728 | tf_op jit(solution)/shard_map/all_gather | solution.py:170
  590.5 183.5 %reduce-scatter.35.cloned.1.call-start = ((), (), s32[]{:S(2)}) async-start(), calls=%async_computation.33 | async-start | bytes 3063808 | tf_op jit(solution)/shard_map/reduce_scatter | solution.py:345
  597.7 178.3 %reduce-scatter.33.cloned.1.call-start = ((), (), s32[]{:S(2)}) async-start(), calls=%async_computation.32 | async-start | bytes 3063808 | tf_op jit(solution)/shard_map/reduce_scatter | solution.py:342
  606.2 222.8 %reduce-scatter.31.cloned.1.call-start = ((), (), s32[]{:S(2)}) async-start(), calls=%async_computation.31 | async-start | bytes 3063808 | tf_op jit(solution)/shard_map/reduce_scatter | solution.py:339
  613.4 275.6 %reduce-scatter.29.cloned.1.call-start = ((), (), s32[]{:S(2)}) async-start(), calls=%async_computation.30 | async-start | bytes 1114112 | tf_op jit(solution)/shard_map/reduce_scatter | solution.py:336
  694.3 255.1 %reduce-scatter.27.cloned.1.call-start = ((), (), s32[]{:S(2)}) async-start(), calls=%async_computation.29 | async-start | bytes 1114112 | tf_op jit(solution)/shard_map/reduce_scatter | solution.py:333
  709.1 300.2 %reduce-scatter.25.cloned.1.call-start = ((), (), s32[]{:S(2)}) async-start(), calls=%async_computation.28 | async-start | bytes 1114112 | tf_op jit(solution)/shard_map/reduce_scatter | solution.py:330
  761.6 308.2 %reduce-scatter.23.cloned.1.call-start = ((), (), s32[]{:S(2)}) async-start(), calls=%async_computation.27 | async-start | bytes 1114112 | tf_op jit(solution)/shard_map/reduce_scatter | solution.py:327
  766.9 336.0 %reduce-scatter.21.cloned.1.call-start = ((), (), s32[]{:S(2)}) async-start(), calls=%async_computation.26 | async-start | bytes 3145728 | tf_op jit(solution)/shard_map/reduce_scatter | solution.py:174
  773.9 329.0 %copy-start.5 = (bf16[512,1024]{1,0:T(8,128)(2,1)S(1)}, bf16[512,1024]{1,0:T(8,128)(2,1)}, u32[]{:S(2)}) copy-start(bf16[512,1024]{1,0:T(8,128)(2,1)} %param.14) | copy-start | bytes 3145732
  773.9 329.0 %copy-start.37 = (f32[1,1024]{1,0:T(1,128)S(1)}, f32[1,1024]{1,0:T(1,128)}, u32[]{:S(2)}) copy-start(f32[1,1024]{1,0:T(1,128)} %copy-done.36) | copy-start | bytes 12292
  773.9 329.0 %copy-start.39 = (f32[512]{0:T(512)S(1)}, f32[512]{0:T(512)}, u32[]{:S(2)}) copy-start(f32[512]{0:T(512)} %copy-done.38) | copy-start | bytes 6148
  774.0 339.1 %copy-start.8 = (f32[512,1024]{1,0:T(8,128)S(1)}, f32[512,1024]{1,0:T(8,128)}, u32[]{:S(2)}) copy-start(f32[512,1024]{1,0:T(8,128)} %copy-done.7) | copy-start | bytes 6291460
  774.0 339.1 %copy-start.40 = (f32[512]{0:T(512)S(1)}, f32[512]{0:T(512)}, u32[]{:S(2)}) copy-start(f32[512]{0:T(512)} %get-tuple-element.129) | copy-start | bytes 6148
  774.0 395.6 %reduce-scatter.37.cloned.1.call-start = ((), (), s32[]{:S(2)}) async-start(), calls=%async_computation.34 | async-start | bytes 278528
  (45 other events, 370.9 us)
Sparse Core Ops, SparseCore 0:
  10.2 40.6 all-gather.18
  53.0 32.0 all-gather.12
  87.2 37.9 all-gather.16
  127.2 36.8 all-gather.14
  166.1 36.8 all-gather.20
  207.7 53.2 reduce-scatter.14
  263.5 44.3 all-gather.24
  310.0 31.4 all-gather.22
  344.1 44.3 all-gather.26
  390.9 42.6 all-gather.28
  441.8 52.6 reduce-scatter.16
  499.6 33.1 all-gather.30
  552.1 31.8 reduce-scatter.18
  590.6 33.0 all-gather.32
  627.9 65.1 reduce-scatter.34
  696.7 64.0 reduce-scatter.32
  765.0 64.0 reduce-scatter.30
  832.5 56.3 reduce-scatter.28
  893.0 56.3 reduce-scatter.26
  952.9 56.4 reduce-scatter.24
  1013.4 56.3 reduce-scatter.22
  1072.1 30.8 reduce-scatter.20
  1113.2 56.3 reduce-scatter.36
where the time goes:
time: 1190 us; the launch traced here: 1180 us
  waiting for transfers between devices  815 us (68%)
  matrix products  230 us (19%)
  other arithmetic  57.2 us (5%)
  blocking collectives  30.1 us (3%)
  local copies, waits for them, and re-layouts  27.9 us (2%)
  between operations  15.2 us (1%)
    reduce_scatter x2, waiting for transfers between devices, sum_rows(): lax.psum_scatter(sum_terms, 'tensor', scatter_dimension=0, tiled=True)  105 us
    all_gather x2, waiting for transfers between devices, gather_rows(): return lax.all_gather(normed, 'tensor', axis=0, tiled=True)  67.9 us
    reduce_scatter x2, waiting for transfers between devices, sum_grads(): lax.psum_scatter(grad_terms.astype(jnp.bfloat16), 'tensor', scatter_dimen...  63.6 us
    reduce_scatter x1, waiting for transfers between devices, on_device(): lax.psum_scatter(weight_terms[0].astype(jnp.bfloat16), 'dp', scatter_dime...  59 us
    reduce_scatter x1, waiting for transfers between devices, on_device(): lax.psum_scatter(weight_terms[2].astype(jnp.bfloat16), 'dp', scatter_dime...  59 us
    reduce_scatter x1, waiting for transfers between devices, on_device(): lax.psum_scatter(weight_terms[1].astype(jnp.bfloat16), 'dp', scatter_dime...  58.4 us
    reduce_scatter x1, waiting for transfers between devices, on_device(): lax.psum_scatter(weight_terms[3].astype(jnp.bfloat16), 'dp', scatter_dime...  58.2 us
    unnamed x24, waiting for transfers between devices  58 us
  transfers between devices with their start and end apart: 23, of which 21 were waited for; matrix products, arithmetic and copies ran while one was open for 22% of the time, Pallas kernels for 0%

commit v1 on v0

--- a/solution.py
+++ b/solution.py
@@ -1,8 +1,11 @@
+import functools
 import math
 
 import jax
 import jax.numpy as jnp
 from jax import lax
+from jax.experimental import pallas as pl
+from jax.experimental.pallas import tpu as pltpu
 from jax.sharding import PartitionSpec as P
 
 HEAD_DIM = 128
@@ -366,6 +369,850 @@
     )
 
 
+LANES = 128
+HALF = HEAD_DIM // 2
+MESH = pl.DeviceIdType.MESH
+f32 = jnp.float32
+bf16 = jnp.bfloat16
+
+
+class Plan:
+    def __init__(self, rows, width, head_cols, ff_cols, shard_rows):
+        self.rows = rows
+        self.width = width
+        self.head_cols = head_cols
+        self.ff_cols = ff_cols
+        self.shard_rows = shard_rows
+        self.heads = 2 * head_cols // HEAD_DIM
+        self.k_at = LANES
+        self.v_at = self.k_at + head_cols
+        self.q_at = self.v_at + head_cols
+        self.o_at = self.q_at + head_cols
+        self.gu_at = self.o_at + head_cols
+        self.d_at = self.gu_at + 2 * ff_cols
+        self.cols = self.d_at + ff_cols
+        self.kvq = 3 * head_cols
+
+        def cuts(start, total):
+            pieces = []
+            while total > 0:
+                size = min(512, total)
+                pieces.append((start, size))
+                start, total = start + size, total - size
+            return pieces
+
+        self.gu_cuts = cuts(self.gu_at, 2 * ff_cols)
+        self.d_cuts = cuts(self.d_at, ff_cols)
+        self.gather = (
+            [(0, LANES + head_cols), (self.v_at, head_cols), (self.q_at, head_cols), (self.o_at, head_cols)]
+            + self.gu_cuts
+            + self.d_cuts
+        )
+        self.reduce = (
+            self.d_cuts
+            + self.gu_cuts
+            + [(self.o_at, head_cols), (self.q_at, head_cols), (self.v_at, head_cols), (self.k_at, head_cols), (0, LANES)]
+        )
+
+
+def sigmoid(v):
+    return 0.5 * jnp.tanh(0.5 * v) + 0.5
+
+
+def dot_nn(left, right):
+    return lax.dot_general(left, right, (((1,), (0,)), ((), ())), preferred_element_type=f32)
+
+
+def dot_nt(left, right):
+    return lax.dot_general(left, right, (((1,), (1,)), ((), ())), preferred_element_type=f32)
+
+
+def dot_tn(left, right):
+    return lax.dot_general(left, right, (((0,), (0,)), ((), ())), preferred_element_type=f32)
+
+
+def fused_layer(
+    plan,
+    shard_ref, tok_hbm, og_hbm, starts_ref, cos_ref, sin_ref,
+    out_hbm, ig_hbm, gr_hbm,
+    W, KVQ, KVp, xo, xp, T, att, ba, mid, bff, nf, GU, HID, BF, TB, LO, MK, gains, dgains, stat_a, stat_b,
+    R1, R2A, R2B, R3A, R3B, R4, ST,
+    ag_s, ag_r, rs_s, rs_r, loc, extra_s, extra_r, credit,
+):
+    p = plan
+    dp = lax.axis_index("dp")
+    y = lax.axis_index("tensor")
+    c = lax.rem(dp, 2)
+    x = lax.rem(dp // 2, 2)
+    z = dp // 4
+    rows, width, hc, ff = p.rows, p.width, p.head_cols, p.ff_cols
+    first = y == 0
+    second = y == 1
+
+    def dev(zz, xx, cc, yy):
+        return (zz * 4 + xx * 2 + cc, yy)
+
+    def up(step):
+        return lax.rem(z + step, 4)
+
+    core_peer = dev(z, x, 1 - c, y)
+    x_peer = dev(z, 1 - x, c, y)
+    y_peer = dev(z, x, c, 1 - y)
+    z_peers = [dev(up(d), x, c, y) for d in (1, 2, 3)]
+    z_sources = [dev(up(4 - d), x, c, y) for d in (1, 2, 3)]
+
+    def remote(src, dst, send, recv, to):
+        return pltpu.make_async_remote_copy(
+            src_ref=src, dst_ref=dst, send_sem=send, recv_sem=recv, device_id=to, device_id_type=MESH
+        )
+
+    def cut(at, size):
+        return pl.ds(at if isinstance(at, int) else pl.multiple_of(at, LANES), size)
+
+    def weight(yy, at, size, zz=None):
+        if zz is None:
+            return W[yy, :, :, :, :, cut(at, size)].reshape(width, size)
+        return W[yy, zz, :, :, :, cut(at, size)].reshape(width // 4, size)
+
+    def put_weight(yy, at, size, value):
+        W[yy, :, :, :, :, cut(at, size)] = value.astype(bf16).reshape(4, 2, 2, p.shard_rows, size)
+
+    def rms(v):
+        return lax.rsqrt(jnp.mean(v * v, axis=-1, keepdims=True) + norm_eps)
+
+    def norm_grad(v, scale, gain, e):
+        weighted = gain * e
+        inner = jnp.mean(v * weighted, axis=-1, keepdims=True)
+        return scale * weighted - v * (scale * scale * scale) * inner
+
+    def by_rows(body, size=64):
+        def step(i, carry):
+            body(pl.ds(pl.multiple_of(i * size, size), size))
+            return carry
+
+        lax.fori_loop(0, rows // size, step, 0)
+
+    def loop(count, body):
+        def step(i, carry):
+            body(i)
+            return carry
+
+        lax.fori_loop(0, count, step, 0)
+
+    def ag(k, m):
+        at, size = p.gather[k]
+        cols = pl.ds(at, size)
+        sem = (ag_s.at[k, m], ag_r.at[k, m])
+        if m < 3:
+            return remote(shard_ref.at[:, cols], W.at[y, z, x, c, :, cols], *sem, z_peers[m])
+        if m == 3:
+            ref = W.at[y, pl.ds(0, 2), x, c, :, cols]
+            return remote(ref, ref, *sem, x_peer)
+        if m == 4:
+            ref = W.at[y, pl.ds(2, 2), x, c, :, cols]
+            return remote(ref, ref, *sem, y_peer)
+        if m == 5:
+            ref = W.at[y, pl.ds(0, 2), :, c, :, cols]
+            return remote(ref, ref, *sem, y_peer)
+        if m == 6:
+            ref = W.at[:, pl.ds(2, 2), x, c, :, cols]
+            return remote(ref, ref, *sem, x_peer)
+        ref = W.at[:, :, :, c, :, cols]
+        return remote(ref, ref, *sem, core_peer)
+
+    n_gather = len(p.gather)
+
+    def ag_step(s):
+        if 0 <= s < n_gather:
+            for m in (0, 1, 2):
+                ag(s, m).wait_recv()
+            ag(s, 3).start()
+            ag(s, 4).start()
+        if 0 <= s - 1 < n_gather:
+            ag(s - 1, 3).wait_recv()
+            ag(s - 1, 5).start()
+            ag(s - 1, 4).wait_recv()
+            ag(s - 1, 6).start()
+        if 0 <= s - 2 < n_gather:
+            ag(s - 2, 5).wait_recv()
+            ag(s - 2, 6).wait_recv()
+            ag(s - 2, 7).start()
+        if 0 <= s - 3 < n_gather:
+            ag(s - 3, 7).wait_recv()
+
+    load_tok = pltpu.make_async_copy(tok_hbm, TB, loc.at[0])
+    load_tok.start()
+    own_w = pltpu.make_async_copy(shard_ref, W.at[y, z, x, c], loc.at[1])
+    own_w.start()
+    barrier = pltpu.get_barrier_semaphore()
+    for peer in [core_peer, x_peer, y_peer] + z_peers:
+        pl.semaphore_signal(barrier, inc=1, device_id=peer, device_id_type=MESH)
+    pl.semaphore_wait(barrier, 6)
+
+    tok_send = remote(tok_hbm, xp, extra_s.at[0], extra_r.at[0], y_peer)
+
+    @pl.when(first)
+    def _():
+        tok_send.start()
+
+    for k in range(n_gather):
+        for m in (0, 1, 2):
+            ag(k, m).start()
+    own_w.wait()
+    load_tok.wait()
+
+    start = starts_ref[0, y] - y * rows
+
+    def build_mask(query_dim):
+        def body(blk):
+            shape = (64, rows)
+            r = lax.broadcasted_iota(jnp.int32, shape, 0) + blk.start
+            s = lax.broadcasted_iota(jnp.int32, shape, 1)
+            q_pos, k_pos = (r, s) if query_dim == 0 else (s, r)
+            inside = (r >= start) & (r < start + PIECE) & (s >= start) & (s < start + PIECE)
+            MK[blk, :] = jnp.where((k_pos <= q_pos) | inside, 0.0, masked)
+
+        by_rows(body)
+
+    build_mask(0)
+    dgains[...] = jnp.zeros_like(dgains)
+
+    for s in range(0, 4):
+        ag_step(s)
+
+    gains[0:8, 0:width] = jnp.transpose(weight(0, 0, LANES).astype(f32))[0:8, :]
+
+    def norm_in(src, dst):
+        def body(blk):
+            t = src[blk, :].astype(f32)
+            dst[blk, :] = (t * rms(t) * gains[0:1, :]).astype(bf16)
+
+        by_rows(body)
+
+    norm_in(TB, xo)
+
+    @pl.when(second)
+    def _():
+        tok_send.wait_recv()
+        norm_in(xp, xp)
+
+    ag_step(4)
+    ag_step(5)
+
+    def rotated(u, place, sign):
+        return u * cos_ref[place, :] + sign * (pltpu.roll(u, HALF, 1) * sin_ref[place, :])
+
+    def project(src, dst, at, place, turn):
+        def run(yy, off):
+            r = dot_nn(src[...], weight(yy, LANES + off, 256))
+            for hh in range(2):
+                u = r[:, hh * HEAD_DIM : (hh + 1) * HEAD_DIM]
+                if turn:
+                    u = rotated(u, place, 1.0)
+                dst[yy, :, cut(off + hh * HEAD_DIM, HEAD_DIM)] = u.astype(bf16)
+
+        per = hc // 256
+        loop(2 * per, lambda i: run(i // per, pl.multiple_of(at + lax.rem(i, per) * 256, 256)))
+
+    own_place = pl.ds(pl.multiple_of(y * rows, rows), rows)
+    old_place = pl.ds(0, rows)
+    project(xo, KVQ, 0, own_place, True)
+    project(xo, KVQ, hc, own_place, False)
+    project(xo, KVQ, 2 * hc, own_place, True)
+
+    @pl.when(second)
+    def _():
+        project(xp, KVp, 0, old_place, True)
+        project(xp, KVp, hc, old_place, False)
+
+    ag_step(6)
+
+    per_y = hc // HEAD_DIM
+    attn_scale = 1.0 / math.sqrt(HEAD_DIM)
+    log2_scale = attn_scale * math.log2(math.e)
+    lane = lax.broadcasted_iota(jnp.int32, (1, LANES), 1)
+
+    def head_at(h):
+        yy = h // per_y
+        off = pl.multiple_of(lax.rem(h, per_y) * HEAD_DIM, HEAD_DIM)
+        return yy, cut(off, HEAD_DIM), cut(off + hc, HEAD_DIM), cut(off + 2 * hc, HEAD_DIM)
+
+    def attend(i, both):
+        h = i // 2
+        blk = pl.ds(pl.multiple_of(lax.rem(i, 2) * (rows // 2), rows // 2), rows // 2)
+        yy, k_at, v_at, q_at = head_at(h)
+        q = KVQ[yy, blk, q_at]
+        s = dot_nt(q, KVQ[yy, :, k_at]) * log2_scale + MK[blk, :]
+        top = jnp.max(s, axis=-1, keepdims=True)
+        if both:
+            s_old = dot_nt(q, KVp[yy, :, k_at]) * log2_scale
+            top = jnp.maximum(top, jnp.max(s_old, axis=-1, keepdims=True))
+        e = jnp.exp2(s - top)
+        total = jnp.sum(e, axis=-1, keepdims=True)
+        if both:
+            e_old = jnp.exp2(s_old - top)
+            total = total + jnp.sum(e_old, axis=-1, keepdims=True)
+        inv = 1.0 / total
+        o = dot_nn((e * inv).astype(bf16), KVQ[yy, :, v_at])
+        if both:
+            o = o + dot_nn((e_old * inv).astype(bf16), KVp[yy, :, v_at])
+        att[blk, pl.ds(pl.multiple_of(h * HEAD_DIM, HEAD_DIM), HEAD_DIM)] = o.astype(bf16)
+        stat = top + jnp.log2(total)
+        stat_a[blk, :] = jnp.where(lane == h, stat, stat_a[blk, :])
+
+    def attend_heads(lo, hi):
+        @pl.when(first)
+        def _():
+            loop(2 * (hi - lo), lambda i: attend(i + 2 * lo, False))
+
+        @pl.when(second)
+        def _():
+            loop(2 * (hi - lo), lambda i: attend(i + 2 * lo, True))
+
+    stat_a[...] = jnp.zeros_like(stat_a)
+    attend_heads(0, p.heads)
+    ag_step(7)
+
+    def o_proj(zz):
+        cols = pl.ds(pl.multiple_of(zz * (width // 4), width // 4), width // 4)
+        ba[:, cols] = dot_nt(att[:, 0:hc], weight(0, p.o_at, hc, zz)) + dot_nt(
+            att[:, hc : 2 * hc], weight(1, p.o_at, hc, zz)
+        )
+
+    loop(4, o_proj)
+
+    def mid_rows(blk):
+        b = ba[blk, :]
+        m = TB[blk, :].astype(f32) + b * rms(b) * gains[1:2, :]
+        mid[blk, :] = m
+        nf[blk, :] = (m * rms(m) * gains[2:3, :]).astype(bf16)
+
+    by_rows(mid_rows)
+    load_og = pltpu.make_async_copy(og_hbm, TB, loc.at[0])
+    load_og.start()
+    ag_step(8)
+
+    def gate_up(lo, hi):
+        def run(i):
+            yy = i // (hi - lo)
+            t = lax.rem(i, hi - lo) + lo
+            off = pl.multiple_of(t * 256, 256)
+            r = dot_nn(nf[...], weight(yy, p.gu_at + off, 256))
+            g, u = r[:, 0:LANES], r[:, LANES:256]
+            GU[yy, :, pl.ds(off, 256)] = r.astype(bf16)
+            HID[yy, :, pl.ds(pl.multiple_of(t * LANES, LANES), LANES)] = (
+                g * sigmoid(g) * u
+            ).astype(bf16)
+
+        loop(2 * (hi - lo), run)
+
+    ag_step(9)
+    gate_up(0, 6)
+    ag_step(10)
+    ag_step(11)
+    ag_step(12)
+    gate_up(6, 2 * ff // 256)
+    for s in range(13, n_gather + 3):
+        ag_step(s)
+
+    def down_proj(zz):
+        cols = pl.ds(pl.multiple_of(zz * (width // 4), width // 4), width // 4)
+        bff[:, cols] = dot_nt(HID[0], weight(0, p.d_at, ff, zz)) + dot_nt(HID[1], weight(1, p.d_at, ff, zz))
+
+    loop(4, down_proj)
+    load_og.wait()
+
+    def out_rows(blk):
+        b = bff[blk, :]
+        scale = rms(b)
+        e = TB[blk, :].astype(f32)
+        LO[blk, :] = (mid[blk, :] + b * scale * gains[3:4, :]).astype(bf16)
+        BF[blk, :] = norm_grad(b, scale, gains[3:4, :], e).astype(bf16)
+        dgains[3:4, :] += jnp.sum(b * scale * e, axis=0, keepdims=True)
+
+    by_rows(out_rows)
+    put_out = pltpu.make_async_copy(LO, out_hbm, loc.at[1])
+    put_out.start()
+
+    for k in range(n_gather):
+        for m in range(8):
+            ag(k, m).wait_send()
+
+    n_reduce = len(p.reduce)
+
+    def rs(j, m):
+        at, size = p.reduce[j]
+        cols, slot, part = pl.ds(at, size), j % 2, pl.ds(0, size)
+        sem = (rs_s.at[j, m], rs_r.at[j, m])
+        low, high = pl.ds(0, 2), pl.ds(2, 2)
+        if m == 0:
+            return remote(W.at[:, :, :, 1 - c, :, cols], R1.at[slot, :, :, :, :, part], *sem, core_peer)
+        if m == 1:
+            return remote(W.at[1 - y, low, :, c, :, cols], R2A.at[slot, :, :, :, part], *sem, y_peer)
+        if m == 2:
+            return remote(W.at[:, high, 1 - x, c, :, cols], R2B.at[slot, :, :, :, part], *sem, x_peer)
+        if m == 3:
+            return remote(W.at[y, low, 1 - x, c, :, cols], R3A.at[slot, :, :, part], *sem, x_peer)
+        if m == 4:
+            return remote(W.at[1 - y, high, x, c, :, cols], R3B.at[slot, :, :, part], *sem, y_peer)
+        d = m - 5
+        return remote(W.at[y, up(d + 1), x, c, :, cols], R4.at[slot, d, :, part], *sem, z_peers[d])
+
+    rs_sources = [core_peer, y_peer, x_peer, x_peer, y_peer] + z_sources
+
+    def rs_start(j, m):
+        if j >= 2:
+            pl.semaphore_wait(credit.at[m], 1)
+        rs(j, m).start()
+
+    def rs_used(j, m):
+        if j + 2 < n_reduce:
+            pl.semaphore_signal(credit.at[m], inc=1, device_id=rs_sources[m], device_id_type=MESH)
+
+    def put_sum(j):
+        at, size = p.reduce[j]
+        return pltpu.make_async_copy(
+            ST.at[j % 2, :, pl.ds(0, size)], gr_hbm.at[:, pl.ds(at, size)], loc.at[2 + j % 2]
+        )
+
+    def rs_event(j, phase):
+        at, size = p.reduce[j]
+        cols, slot, part = pl.ds(at, size), j % 2, pl.ds(0, size)
+        if phase == 0:
+            rs_start(j, 0)
+        elif phase == 1:
+            rs(j, 0).wait_recv()
+
+            def add(i):
+                a, b, d = i // 8, lax.rem(i // 2, 4), lax.rem(i, 2)
+                W[a, b, d, c, :, cols] = W[a, b, d, c, :, cols] + R1[slot, a, b, d, :, part]
+
+            loop(16, add)
+            rs_used(j, 0)
+            rs_start(j, 1)
+            rs_start(j, 2)
+        elif phase == 2:
+            rs(j, 1).wait_recv()
+
+            def add_a(i):
+                b, d = i // 2, lax.rem(i, 2)
+                W[y, b, d, c, :, cols] = W[y, b, d, c, :, cols] + R2A[slot, b, d, :, part]
+
+            loop(4, add_a)
+            rs_used(j, 1)
+            rs_start(j, 3)
+            rs(j, 2).wait_recv()
+
+            def add_b(i):
+                a, b = i // 2, lax.rem(i, 2)
+                W[a, b + 2, x, c, :, cols] = W[a, b + 2, x, c, :, cols] + R2B[slot, a, b, :, part]
+
+            loop(4, add_b)
+            rs_used(j, 2)
+            rs_start(j, 4)
+        elif phase == 3:
+            rs(j, 3).wait_recv()
+            rs(j, 4).wait_recv()
+            for b in range(2):
+                W[y, b, x, c, :, cols] = W[y, b, x, c, :, cols] + R3A[slot, b, :, part]
+                W[y, b + 2, x, c, :, cols] = W[y, b + 2, x, c, :, cols] + R3B[slot, b, :, part]
+            rs_used(j, 3)
+            rs_used(j, 4)
+            for m in (5, 6, 7):
+                rs_start(j, m)
+        else:
+            for m in (5, 6, 7):
+                rs(j, m).wait_recv()
+            if j >= 2:
+                put_sum(j - 2).wait()
+            total = W[y, z, x, c, :, cols].astype(f32)
+            for d in range(3):
+                total = total + R4[slot, d, :, part].astype(f32)
+            ST[slot, :, part] = total
+            for m in (5, 6, 7):
+                rs_used(j, m)
+            put_sum(j).start()
+
+    events = [(j, t - j) for t in range(n_reduce + 4) for j in range(n_reduce) if 0 <= t - j <= 4]
+    done = [0]
+
+    def pump(ready, until):
+        while done[0] < len(events):
+            j, phase = events[done[0]]
+            if j >= ready or j + phase >= until:
+                break
+            rs_event(j, phase)
+            done[0] += 1
+
+    def back_tile(yy, t, bh):
+        off = pl.multiple_of(t * 256, 256)
+        g = GU[yy, :, pl.ds(off, LANES)].astype(f32)
+        u = GU[yy, :, cut(off + LANES, LANES)].astype(f32)
+        s = sigmoid(g)
+        GU[yy, :, pl.ds(off, LANES)] = (bh * u * s * (1.0 + g * (1.0 - s))).astype(bf16)
+        GU[yy, :, cut(off + LANES, LANES)] = (bh * g * s).astype(bf16)
+
+    pairs = ff // 256
+
+    def back_pair(i):
+        yy, t = i // pairs, lax.rem(i, pairs)
+        bh = dot_nn(BF[...], weight(yy, p.d_at + pl.multiple_of(t * 256, 256), 256))
+        back_tile(yy, 2 * t, bh[:, 0:LANES])
+        back_tile(yy, 2 * t + 1, bh[:, LANES:256])
+
+    def back_last(yy):
+        bh = dot_nn(BF[...], weight(yy, p.d_at + pairs * 256, LANES))
+        back_tile(yy, jnp.int32(2 * pairs), bh)
+
+    loop(2 * pairs, back_pair)
+    if ff % 256:
+        loop(2, back_last)
+
+    T[...] = jnp.transpose(BF[...])
+
+    def grad_down_pair(i):
+        yy, off = i // pairs, pl.multiple_of(lax.rem(i, pairs) * 256, 256)
+        put_weight(yy, p.d_at + off, 256, dot_nn(T[...], HID[yy, :, pl.ds(off, 256)]))
+
+    def grad_down_last(yy):
+        put_weight(yy, p.d_at + pairs * 256, LANES, dot_nn(T[...], HID[yy, :, pl.ds(pairs * 256, LANES)]))
+
+    loop(2 * pairs, grad_down_pair)
+    if ff % 256:
+        loop(2, grad_down_last)
+
+    n_d = len(p.d_cuts)
+    n_gu = n_d + len(p.gu_cuts)
+    pump(n_d, 2)
+
+    def back_normed(zz):
+        cols = pl.ds(pl.multiple_of(zz * (width // 4), width // 4), width // 4)
+        acc = dot_nt(GU[0, :, 0:ff], weight(0, p.gu_at, ff, zz))
+        acc = acc + dot_nt(GU[0, :, ff : 2 * ff], weight(0, p.gu_at + ff, ff, zz))
+        acc = acc + dot_nt(GU[1, :, 0:ff], weight(1, p.gu_at, ff, zz))
+        bff[:, cols] = acc + dot_nt(GU[1, :, ff : 2 * ff], weight(1, p.gu_at + ff, ff, zz))
+
+    loop(4, back_normed)
+    pump(n_d, 4)
+    T[...] = jnp.transpose(nf[...])
+
+    def grad_gate_up(lo, hi):
+        def run(i):
+            yy, off = i // (hi - lo), pl.multiple_of((lax.rem(i, hi - lo) + lo) * 256, 256)
+            put_weight(yy, p.gu_at + off, 256, dot_nn(T[...], GU[yy, :, pl.ds(off, 256)]))
+
+        loop(2 * (hi - lo), run)
+
+    grad_gate_up(0, 4)
+    pump(n_d + 2, 5)
+    grad_gate_up(4, 2 * ff // 256)
+    pump(n_gu, 6)
+
+    def mid_back(blk):
+        m = mid[blk, :]
+        scale = rms(m)
+        e = bff[blk, :]
+        bm = TB[blk, :].astype(f32) + norm_grad(m, scale, gains[2:3, :], e)
+        dgains[2:3, :] += jnp.sum(m * scale * e, axis=0, keepdims=True)
+        b = ba[blk, :]
+        scale_b = rms(b)
+        BF[blk, :] = norm_grad(b, scale_b, gains[1:2, :], bm).astype(bf16)
+        dgains[1:2, :] += jnp.sum(b * scale_b * bm, axis=0, keepdims=True)
+        mid[blk, :] = bm
+
+    by_rows(mid_back)
+    load_again = pltpu.make_async_copy(tok_hbm, TB, loc.at[0])
+    load_again.start()
+    pump(n_gu, 7)
+
+    per_o = hc // 256
+
+    def back_att(i):
+        yy, off = i // per_o, pl.multiple_of(lax.rem(i, per_o) * 256, 256)
+        nf[:, cut(yy * hc + off, 256)] = dot_nn(BF[...], weight(yy, p.o_at + off, 256)).astype(bf16)
+
+    loop(2 * per_o, back_att)
+    T[...] = jnp.transpose(BF[...])
+
+    def grad_out_tile(i):
+        yy, off = i // per_o, pl.multiple_of(lax.rem(i, per_o) * 256, 256)
+        put_weight(yy, p.o_at + off, 256, dot_nn(T[...], att[:, cut(yy * hc + off, 256)]))
+
+    loop(2 * per_o, grad_out_tile)
+    pump(n_gu + 1, 8)
+
+    stat_b[...] = jnp.zeros_like(stat_b)
+    for h in range(p.heads):
+        cols = slice(h * HEAD_DIM, (h + 1) * HEAD_DIM)
+        inner = jnp.sum(nf[:, cols].astype(f32) * att[:, cols].astype(f32), axis=-1, keepdims=True)
+        stat_b[...] = jnp.where(lane == h, inner, stat_b[...])
+    log_rows = jnp.transpose(stat_a[...])[0 : p.heads, :]
+    inner_rows = jnp.transpose(stat_b[...])[0 : p.heads, :]
+    gains[8 : 8 + p.heads, 0:rows] = log_rows
+    gains[8 : 8 + p.heads, rows : 2 * rows] = inner_rows
+    build_mask(1)
+
+    def attend_grad(h, both):
+        yy, k_at, v_at, q_at = head_at(h)
+        q = KVQ[yy, :, q_at]
+        do = nf[:, pl.ds(pl.multiple_of(h * HEAD_DIM, HEAD_DIM), HEAD_DIM)]
+        log_row = gains[pl.ds(8 + h, 1), 0:rows]
+        inner_row = gains[pl.ds(8 + h, 1), rows : 2 * rows]
+
+        def side(ref, place, hide):
+            k, v = ref[yy, :, k_at], ref[yy, :, v_at]
+            s = dot_nt(k, q) * log2_scale
+            if hide:
+                s = s + MK[...]
+            prob = jnp.exp2(s - log_row)
+            dv = dot_nn(prob.astype(bf16), do)
+            ds = (prob * (dot_nt(v, do) - inner_row) * attn_scale).astype(bf16)
+            dk = dot_nn(ds, q)
+            dq = dot_tn(ds, k)
+            ref[yy, :, v_at] = dv.astype(bf16)
+            ref[yy, :, k_at] = rotated(dk, place, -1.0).astype(bf16)
+            return dq
+
+        dq = side(KVQ, own_place, True)
+        if both:
+            dq = dq + side(KVp, old_place, False)
+        KVQ[yy, :, q_at] = rotated(dq, own_place, -1.0).astype(bf16)
+
+    def grad_heads(lo, hi):
+        @pl.when(first)
+        def _():
+            loop(hi - lo, lambda h: attend_grad(h + lo, False))
+
+        @pl.when(second)
+        def _():
+            loop(hi - lo, lambda h: attend_grad(h + lo, True))
+
+    half_heads = p.heads // 2
+    grad_heads(0, half_heads)
+    pump(n_gu + 1, 10)
+    grad_heads(half_heads, p.heads)
+    pump(n_gu + 1, 11)
+    put_out.wait()
+
+    back_send = remote(LO, KVp.at[0, :, pl.ds(0, width)], extra_s.at[1], extra_r.at[1], y_peer)
+
+    @pl.when(second)
+    def _():
+        def old_back(zz):
+            cols = pl.ds(pl.multiple_of(zz * (width // 4), width // 4), width // 4)
+            LO[:, cols] = (
+                dot_nt(KVp[0], weight(0, p.k_at, 2 * hc, zz)) + dot_nt(KVp[1], weight(1, p.k_at, 2 * hc, zz))
+            ).astype(bf16)
+
+        loop(4, old_back)
+        back_send.start()
+
+    def own_back(zz):
+        cols = pl.ds(pl.multiple_of(zz * (width // 4), width // 4), width // 4)
+        bff[:, cols] = dot_nt(KVQ[0], weight(0, p.k_at, p.kvq, zz)) + dot_nt(KVQ[1], weight(1, p.k_at, p.kvq, zz))
+
+    loop(4, own_back)
+    pump(n_gu + 1, 12)
+    T[...] = jnp.transpose(xo[...])
+    tiles = p.kvq // 256
+
+    def grad_kvq(i):
+        yy, off = i // tiles, pl.multiple_of(lax.rem(i, tiles) * 256, 256)
+        put_weight(yy, p.k_at + off, 256, dot_nn(T[...], KVQ[yy, :, pl.ds(off, 256)]))
+
+    loop(2 * tiles, grad_kvq)
+
+    @pl.when(second)
+    def _():
+        T[...] = jnp.transpose(xp[...])
+        old_tiles = 2 * hc // 256
+
+        def grad_old(i):
+            yy, off = i // old_tiles, pl.multiple_of(lax.rem(i, old_tiles) * 256, 256)
+            put_weight(
+                yy, p.k_at + off, 256,
+                weight(yy, p.k_at + off, 256).astype(f32) + dot_nn(T[...], KVp[yy, :, pl.ds(off, 256)]),
+            )
+
+        loop(2 * old_tiles, grad_old)
+
+    pump(n_reduce - 1, 13)
+    load_again.wait()
+
+    @pl.when(first)
+    def _():
+        back_send.wait_recv()
+
+        def join(blk):
+            bff[blk, :] += KVp[0, blk, pl.ds(0, width)].astype(f32)
+
+        by_rows(join)
+
+    def in_back(blk):
+        t = TB[blk, :].astype(f32)
+        scale = rms(t)
+        e = bff[blk, :]
+        mid[blk, :] = mid[blk, :] + norm_grad(t, scale, gains[0:1, :], e)
+        dgains[0:1, :] += jnp.sum(t * scale * e, axis=0, keepdims=True)
+
+    by_rows(in_back)
+    put_ig = pltpu.make_async_copy(mid, ig_hbm, loc.at[0])
+    put_ig.start()
+
+    gain_cols = jnp.transpose(jnp.concatenate([dgains[...], jnp.zeros((LANES - 8, width), f32)], axis=0))
+    put_weight(0, 0, LANES, gain_cols)
+    put_weight(1, 0, LANES, gain_cols)
+    pump(n_reduce, len(events))
+    put_ig.wait()
+    for j in (n_reduce - 2, n_reduce - 1):
+        put_sum(j).wait()
+
+    for j in range(n_reduce):
+        for m in range(8):
+            rs(j, m).wait_send()
+
+    @pl.when(first)
+    def _():
+        tok_send.wait_send()
+
+    @pl.when(second)
+    def _():
+        back_send.wait_send()
+
+
+def pack_rows(plan, weights, gain_shards):
+    query, key, value, out, gate, up, down = weights
+    shard_rows = plan.shard_rows
+    columns = jnp.stack(gain_shards, axis=1)
+    columns = jnp.pad(columns, ((0, 0), (0, LANES - columns.shape[1])))
+    turns = jnp.stack(
+        [gate.reshape(shard_rows, -1, LANES), up.reshape(shard_rows, -1, LANES)], axis=2
+    ).reshape(shard_rows, -1)
+    return jnp.concatenate([columns, key, value, query, out.T, turns, down.T], axis=1)
+
+
+def unpack_rows(plan, total):
+    hc, ff = plan.head_cols, plan.ff_cols
+
+    def piece(at, size):
+        return total[:, at : at + size]
+
+    turns = piece(plan.gu_at, 2 * ff).reshape(plan.shard_rows, -1, 2, LANES)
+    return (
+        piece(plan.q_at, hc),
+        piece(plan.k_at, hc),
+        piece(plan.v_at, hc),
+        piece(plan.o_at, hc).T,
+        turns[:, :, 0].reshape(plan.shard_rows, ff),
+        turns[:, :, 1].reshape(plan.shard_rows, ff),
+        piece(plan.d_at, ff).T,
+        total[:, 0],
+        total[:, 1],
+        total[:, 2],
+        total[:, 3],
+    )
+
+
+def fused_on_device(
+    tokens,
+    query_weight,
+    key_weight,
+    value_weight,
+    out_weight,
+    gate_weight,
+    up_weight,
+    down_weight,
+    gain_attn_in,
+    gain_attn_out,
+    gain_ff_in,
+    gain_ff_out,
+    piece_starts,
+    out_grad,
+):
+    rows, width = tokens.shape
+    plan = Plan(rows, width, query_weight.shape[1], gate_weight.shape[1], query_weight.shape[0])
+    shard = pack_rows(
+        plan,
+        (query_weight, key_weight, value_weight, out_weight, gate_weight, up_weight, down_weight),
+        (gain_attn_in, gain_attn_out, gain_ff_in, gain_ff_out),
+    )
+    cosine, sine = rope_at(jnp.arange(2 * rows, dtype=jnp.int32))
+    cosine, sine = cosine[:, 0], sine[:, 0]
+    cos_table = jnp.concatenate([cosine, cosine], axis=1)
+    sin_table = jnp.concatenate([-sine, sine], axis=1)
+    hc, ff, sr = plan.head_cols, plan.ff_cols, plan.shard_rows
+    anywhere = pl.BlockSpec(memory_space=pl.ANY)
+    in_vmem = pl.BlockSpec(memory_space=pltpu.VMEM)
+    n_gather, n_reduce = len(plan.gather), len(plan.reduce)
+    scratch = [
+        pltpu.VMEM((2, 4, 2, 2, sr, plan.cols), bf16),
+        pltpu.VMEM((2, rows, 3 * hc), bf16),
+        pltpu.VMEM((2, rows, 2 * hc), bf16),
+        pltpu.VMEM((rows, width), bf16),
+        pltpu.VMEM((rows, width), bf16),
+        pltpu.VMEM((width, rows), bf16),
+        pltpu.VMEM((rows, 2 * hc), bf16),
+        pltpu.VMEM((rows, width), f32),
+        pltpu.VMEM((rows, width), f32),
+        pltpu.VMEM((rows, width), f32),
+        pltpu.VMEM((rows, width), bf16),
+        pltpu.VMEM((2, rows, 2 * ff), bf16),
+        pltpu.VMEM((2, rows, ff), bf16),
+        pltpu.VMEM((rows, width), bf16),
+        pltpu.VMEM((rows, width), bf16),
+        pltpu.VMEM((rows, width), bf16),
+        pltpu.VMEM((rows, rows), f32),
+        pltpu.VMEM((8 + plan.heads, max(width, 2 * rows)), f32),
+        pltpu.VMEM((8, width), f32),
+        pltpu.VMEM((rows, LANES), f32),
+        pltpu.VMEM((rows, LANES), f32),
+        pltpu.VMEM((2, 2, 4, 2, sr, 512), bf16),
+        pltpu.VMEM((2, 2, 2, sr, 512), bf16),
+        pltpu.VMEM((2, 2, 2, sr, 512), bf16),
+        pltpu.VMEM((2, 2, sr, 512), bf16),
+        pltpu.VMEM((2, 2, sr, 512), bf16),
+        pltpu.VMEM((2, 3, sr, 512), bf16),
+        pltpu.VMEM((2, sr, 512), f32),
+        pltpu.SemaphoreType.DMA((n_gather, 8)),
+        pltpu.SemaphoreType.DMA((n_gather, 8)),
+        pltpu.SemaphoreType.DMA((n_reduce, 8)),
+        pltpu.SemaphoreType.DMA((n_reduce, 8)),
+        pltpu.SemaphoreType.DMA((4,)),
+        pltpu.SemaphoreType.DMA((2,)),
+        pltpu.SemaphoreType.DMA((2,)),
+        pltpu.SemaphoreType.REGULAR((8,)),
+    ]
+    out, input_grad, total = pl.pallas_call(
+        functools.partial(fused_layer, plan),
+        out_shape=(
+            jax.ShapeDtypeStruct((rows, width), bf16),
+            jax.ShapeDtypeStruct((rows, width), f32),
+            jax.ShapeDtypeStruct((sr, plan.cols), f32),
+        ),
+        in_specs=[anywhere, anywhere, anywhere, pl.BlockSpec(memory_space=pltpu.SMEM), in_vmem, in_vmem],
+        out_specs=(anywhere, anywhere, anywhere),
+        scratch_shapes=scratch,
+        compiler_params=pltpu.CompilerParams(
+            collective_id=0, has_side_effects=True, vmem_limit_bytes=67043328
+        ),
+        name="fused_layer",
+    )(shard, tokens, out_grad, piece_starts, cos_table, sin_table)
+    return (out, input_grad) + unpack_rows(plan, total)
+
+
+def fits_fused(mesh, tokens, query_weight, gate_weight, piece_starts):
+    dp, tensor = mesh.shape["dp"], mesh.shape["tensor"]
+    sequences, pieces = piece_starts.shape
+    return (
+        (dp, tensor, pieces, sequences) == (16, 2, 2, dp)
+        and tokens.shape[0] % (dp * tensor * 256) == 0
+        and tokens.shape[1] == query_weight.shape[1]
+        and tokens.shape[1] % (dp * 16) == 0
+        and query_weight.shape[1] % (tensor * 256) == 0
+        and gate_weight.shape[1] % (tensor * LANES) == 0
+    )
+
+
 def solution(mesh):
     placed = (
         P(("dp", "tensor"), None),
@@ -383,24 +1230,31 @@
         P("dp", None),
         P(("dp", "tensor"), None),
     )
-    return jax.shard_map(
-        on_device,
-        mesh=mesh,
-        in_specs=placed,
-        out_specs=(
-            P(("dp", "tensor"), None),
-            P(("dp", "tensor"), None),
-            P("dp", "tensor"),
-            P("dp", "tensor"),
-            P("dp", "tensor"),
-            P("tensor", "dp"),
-            P("dp", "tensor"),
-            P("dp", "tensor"),
-            P("tensor", "dp"),
-            P("dp"),
-            P("dp"),
-            P("dp"),
-            P("dp"),
-        ),
-        check_vma=False,
-    )
+    def step(*arrays):
+        fused = fits_fused(mesh, arrays[0], arrays[1], arrays[5], arrays[12])
+        return place(fused_on_device if fused else on_device)(*arrays)
+
+    def place(body):
+        return jax.shard_map(
+            body,
+            mesh=mesh,
+            in_specs=placed,
+            out_specs=(
+                P(("dp", "tensor"), None),
+                P(("dp", "tensor"), None),
+                P("dp", "tensor"),
+                P("dp", "tensor"),
+                P("dp", "tensor"),
+                P("tensor", "dp"),
+                P("dp", "tensor"),
+                P("dp", "tensor"),
+                P("tensor", "dp"),
+                P("dp"),
+                P("dp"),
+                P("dp"),
+                P("dp"),
+            ),
+            check_vma=False,
+        )
+
+    return step

time: 1190 us -> 346 us (0.29); the launches traced: 1180 us -> 346 us
  waiting for transfers between devices: 815 us -> 0 us
  Pallas kernels: 0 us -> 321 us
  matrix products: 230 us -> 0 us
  other arithmetic: 57.2 us -> 4.07 us
  blocking collectives: 30.1 us -> 0 us
  between operations: 15.2 us -> 0.77 us
    reduce_scatter x11 -> x0, waiting for transfers between devices: 455 us -> none  [the longest x2 105 us: sum_rows(): lax.psum_scatter(sum_terms, 'tensor', scatter_dimension=0, tiled=True)]
    pallas_call x0 -> x1, Pallas kernels: none -> 321 us  [fused_on_device(): pl.pallas_call(functools.partial(fused_layer, plan), out_shape=(jax.Shape...]
    all_gather x11 -> x0, waiting for transfers between devices: 302 us -> none  [the longest x2 67.9 us: gather_rows(): return lax.all_gather(normed, 'tensor', axis=0, tiled=True)]
    dot_general x33 -> x0, matrix products: 230 us -> none  [the longest x2 47.9 us: attend_back(): jnp.einsum('hqk,qhd->khd', grad_scores, q_block, preferred_element_type=j...]
    unnamed x24 -> x0, waiting for transfers between devices: 58 us -> none
    all_gather x1 -> x0, blocking collectives: 23.1 us -> none  [fetch_weights(): lax.all_gather(shards[7], 'dp', axis=1, tiled=True)]
    convert_element_type x13 -> x0, other arithmetic: 18.5 us -> none  [the longest x8 11.2 us: on_device(): grad_sums = (lax.psum_scatter(weight_terms[0].astype(jnp.bfloat16), 'dp',...]
    reduce_sum x11 -> x0, other arithmetic: 17.6 us -> none  [the longest x4 6.49 us: norm_back(): return (backward, jnp.sum(values * scale * incoming, axis=0))]
  transfers between devices with their start and end apart: 23 -> 0, of which waited for: 21 -> 0; matrix products, arithmetic and copies ran while one was open for 22% -> 0% of each run, Pallas kernels for 0% -> 0%
where the time goes in v1:
time: 346 us
  Pallas kernels  321 us (93%)
  local copies, waits for them, and re-layouts  20.2 us (6%)
  other arithmetic  4.07 us (1%)
    pallas_call x1, Pallas kernels, fused_on_device(): pl.pallas_call(functools.partial(fused_layer, plan), out_shape=(jax.Shape...  321 us
    unnamed x24, local copies, waits for them, and re-layouts  7.93 us

profile of v1, /device:TPU:0, one launch (start us, length us, event | category | flops | bytes accessed | tf_op | source)
XLA Modules:
  0.0 346.1 jit_solution(15855305510679711862)
XLA Ops:
  0.7 0.7 pad_maximum_fusion.3
  1.4 0.1 copy.38
  1.5 1.1 stack_reshape.6
  2.6 0.0 copy-start.3
  2.6 0.0 copy-start.4
  2.6 0.0 copy-start.5
  2.6 1.1 stack_reshape.7
  3.7 0.0 copy-start.6
  3.7 0.1 pad_maximum_fusion
  3.8 0.0 copy-start.2
  3.8 0.4 copy.39
  4.2 0.1 reshape.74
  4.4 0.6 constant_dynamic-update-slice_fusion.4
  5.0 0.6 constant_dynamic-update-slice_fusion.3
  5.6 0.6 constant_dynamic-update-slice_fusion.2
  6.3 0.6 constant_dynamic-update-slice_fusion.1
  6.9 0.6 bitcast_dynamic-update-slice_fusion.1
  7.5 0.8 constant_dynamic-update-slice_fusion
  8.3 0.7 bitcast_dynamic-update-slice_fusion.shard_ref
  9.0 1.9 fusion
  10.9 1.3 pad_maximum_fusion.1
  12.2 321.0 %fused_layer.1 = (bf16[512,1024]{1,0:T(8,128)(2,1)}, f32[512,1024]{1,0:T(8,128)}, f32[64,6400]{1,0:T(8,128)}) custom-call(bf16[64,6400]{1,0:T(8,128)(2,1)} %bitcast_dynamic-update-slice_fusion.shard_ref, bf16[512,1024]{1,0:T(8,128)(2,1)} %tok_hbm.1, bf16[512,1024]{1,0:T(8,128)(2,1)} %og_hbm.1, s32[1,2]{1,0:T(1,128)} %starts_ref.1, ...), custom_call_target="tpu_custom_call" | custom-call | tf_op jit(solution)/shard_map/fused_layer/pallas_call | solution.py:1185
  333.3 1.7 slice_reduce_fusion.2
  334.9 1.7 slice_bitcast_fusion
  336.7 1.9 slice_bitcast_fusion.1
  338.6 1.2 slice.40
  339.7 0.4 reshape.75
  340.1 1.9 slice_reduce_fusion
  342.1 0.8 copy.44
  342.9 0.8 copy.45
  343.8 1.0 copy.54
  344.7 1.3 copy.55
  (11 shorter events, 0.0 us)
Async XLA Ops:
  2.6 2.4 copy-start.3
  2.6 3.1 copy-start.4
  2.6 3.7 %copy-start.5 = (bf16[64,512]{1,0:T(8,128)(2,1)S(1)}, bf16[64,512]{1,0:T(8,128)(2,1)}, u32[]{:S(2)}) copy-start(bf16[64,512]{1,0:T(8,128)(2,1)} %param.15) | copy-start | bytes 196612
  3.7 3.2 copy-start.6
  3.8 4.5 %copy-start.2 = (bf16[1408,64]{0,1:T(8,128)(2,1)S(1)}, bf16[1408,64]{0,1:T(8,128)(2,1)}, u32[]{:S(2)}) copy-start(bf16[1408,64]{0,1:T(8,128)(2,1)} %param.21) | copy-start | bytes 540676
  340.1 3.7 %copy-start.1 = (bf16[512,1024]{1,0:T(8,128)(2,1)S(1)}, bf16[512,1024]{1,0:T(8,128)(2,1)}, u32[]{:S(2)}) copy-start(bf16[512,1024]{1,0:T(8,128)(2,1)} %get-tuple-element.47) | copy-start | bytes 3145732
  342.9 1.8 copy-start

commit v2 on v1

--- a/solution.py
+++ b/solution.py
@@ -3,6 +3,7 @@
 
 import jax
 import jax.numpy as jnp
+import numpy as np
 from jax import lax
 from jax.experimental import pallas as pl
 from jax.experimental.pallas import tpu as pltpu
@@ -372,6 +373,18 @@
 LANES = 128
 HALF = HEAD_DIM // 2
 MESH = pl.DeviceIdType.MESH
+GATHER_FIRST = (256, 384)
+GATHER_DOWN = (384, 256, 512, 256)
+REDUCE_DOWN = (512, 512)
+REDUCE_LAST = (256, 256)
+GATHER_LATE = 2
+REDUCE_LATE = 0
+LATE_SLOTS = (0, 1, 6, 7, 8)
+X_FIRST = (1, 2)
+X_FIRST_SUM = (2, 2, 2, 2, 2, 2, 2, 2, 1, 1, 1, 1, 1, 1, 1, 1, 1, 1, 1, 1)
+PACE = (1, 2, 3, 4, 5, 6, 7, 8, 9, 10, 11, 12, 13)
+TOKEN_PIECES = 8
+TOKENS_A_STEP = 2
 f32 = jnp.float32
 bf16 = jnp.bfloat16
 
@@ -393,26 +406,41 @@
         self.cols = self.d_at + ff_cols
         self.kvq = 3 * head_cols
 
-        def cuts(start, total):
+        def cuts(start, total, sizes=()):
             pieces = []
             while total > 0:
-                size = min(512, total)
+                size = min(sizes[len(pieces)] if len(pieces) < len(sizes) else 512, total)
                 pieces.append((start, size))
                 start, total = start + size, total - size
             return pieces
 
-        self.gu_cuts = cuts(self.gu_at, 2 * ff_cols)
-        self.d_cuts = cuts(self.d_at, ff_cols)
+        gu_cuts = cuts(self.gu_at, 2 * ff_cols)
         self.gather = (
-            [(0, LANES + head_cols), (self.v_at, head_cols), (self.q_at, head_cols), (self.o_at, head_cols)]
-            + self.gu_cuts
-            + self.d_cuts
+            cuts(0, self.v_at, GATHER_FIRST)
+            + [(self.v_at, head_cols), (self.q_at, head_cols), (self.o_at, head_cols)]
+            + gu_cuts
+            + cuts(self.d_at, ff_cols, GATHER_DOWN)
         )
+        self.d_cuts = cuts(self.d_at, ff_cols, REDUCE_DOWN)
+        self.gu_cuts = gu_cuts
         self.reduce = (
             self.d_cuts
             + self.gu_cuts
-            + [(self.o_at, head_cols), (self.q_at, head_cols), (self.v_at, head_cols), (self.k_at, head_cols), (0, LANES)]
+            + [(self.o_at, head_cols), (self.q_at, head_cols), (self.v_at, head_cols)]
+            + cuts(self.k_at, head_cols, REDUCE_LAST)
+            + [(0, LANES)]
         )
+        self.gather_late = set(range(len(self.gather) - GATHER_LATE, len(self.gather)))
+        self.reduce_late = set(range(REDUCE_LATE))
+
+    def held(self, at):
+        return next(k for k, (start, size) in enumerate(self.gather) if start + size >= at) + 3
+
+    def split(self, k):
+        return X_FIRST[k % len(X_FIRST)]
+
+    def split_sum(self, j):
+        return X_FIRST_SUM[j % len(X_FIRST_SUM)]
 
 
 def sigmoid(v):
@@ -433,11 +461,11 @@
 
 def fused_layer(
     plan,
-    shard_ref, tok_hbm, og_hbm, starts_ref, cos_ref, sin_ref,
+    k_hbm, v_hbm, q_hbm, g_hbm, u_hbm, o_hbm, d_hbm, gain_shard, tok_hbm, og_hbm, starts_ref, inverse_ref,
     out_hbm, ig_hbm, gr_hbm,
-    W, KVQ, KVp, xo, xp, T, att, ba, mid, bff, nf, GU, HID, BF, TB, LO, MK, gains, dgains, stat_a, stat_b,
-    R1, R2A, R2B, R3A, R3B, R4, ST,
-    ag_s, ag_r, rs_s, rs_r, loc, extra_s, extra_r, credit,
+    W, KVQ, KVp, xo, xp, T, att, ba, mid, bff, nf, GU, HID, BF, TB, LO, MK, gains, dgains, stat_a, stat_b, DQ, cos_ref, sin_ref,
+    R1, R2A, R2B, R3A, R3B, R4, RQ1, RQ2, RQ3, ST,
+    ag_s, ag_r, rs_s, rs_r, loc, pack_sem, extra_s, extra_r, credit,
 ):
     p = plan
     dp = lax.axis_index("dp")
@@ -499,67 +527,154 @@
 
         lax.fori_loop(0, count, step, 0)
 
+    own_w = W.at[y, z, x, c]
+
     def ag(k, m):
         at, size = p.gather[k]
         cols = pl.ds(at, size)
         sem = (ag_s.at[k, m], ag_r.at[k, m])
+        if k in p.gather_late:
+            half = size // 2 // LANES * LANES
+            cols_a, cols_b = pl.ds(at, half), pl.ds(at + half, size - half)
+            if m < 3:
+                ref = W.at[:, z, :, c, :, cols]
+                return remote(ref, ref, *sem, z_peers[m])
+            if m == 3:
+                return remote(own_w.at[:, cols_a], W.at[y, z, x, c, :, cols_a], *sem, x_peer)
+            if m == 4:
+                return remote(own_w.at[:, cols_b], W.at[y, z, x, c, :, cols_b], *sem, y_peer)
+            if m == 5:
+                ref = W.at[y, z, :, c, :, cols_a]
+                return remote(ref, ref, *sem, y_peer)
+            if m == 6:
+                ref = W.at[:, z, x, c, :, cols_b]
+                return remote(ref, ref, *sem, x_peer)
+        low, high = pl.ds(0, p.split(k)), pl.ds(p.split(k), 4 - p.split(k))
         if m < 3:
-            return remote(shard_ref.at[:, cols], W.at[y, z, x, c, :, cols], *sem, z_peers[m])
+            return remote(own_w.at[:, cols], W.at[y, z, x, c, :, cols], *sem, z_peers[m])
         if m == 3:
-            ref = W.at[y, pl.ds(0, 2), x, c, :, cols]
+            ref = W.at[y, low, x, c, :, cols]
             return remote(ref, ref, *sem, x_peer)
         if m == 4:
-            ref = W.at[y, pl.ds(2, 2), x, c, :, cols]
+            ref = W.at[y, high, x, c, :, cols]
             return remote(ref, ref, *sem, y_peer)
         if m == 5:
-            ref = W.at[y, pl.ds(0, 2), :, c, :, cols]
+            ref = W.at[y, low, :, c, :, cols]
             return remote(ref, ref, *sem, y_peer)
         if m == 6:
-            ref = W.at[:, pl.ds(2, 2), x, c, :, cols]
+            ref = W.at[:, high, x, c, :, cols]
             return remote(ref, ref, *sem, x_peer)
         ref = W.at[:, :, :, c, :, cols]
         return remote(ref, ref, *sem, core_peer)
 
     n_gather = len(p.gather)
+    n_early = n_gather - len(p.gather_late)
 
     def ag_step(s):
-        if 0 <= s < n_gather:
+        if 0 <= s < n_early:
             for m in (0, 1, 2):
                 ag(s, m).wait_recv()
             ag(s, 3).start()
             ag(s, 4).start()
-        if 0 <= s - 1 < n_gather:
+        if 0 <= s - 1 < n_early:
             ag(s - 1, 3).wait_recv()
             ag(s - 1, 5).start()
             ag(s - 1, 4).wait_recv()
             ag(s - 1, 6).start()
-        if 0 <= s - 2 < n_gather:
+        if 0 <= s - 2 < n_early:
             ag(s - 2, 5).wait_recv()
             ag(s - 2, 6).wait_recv()
             ag(s - 2, 7).start()
-        if 0 <= s - 3 < n_gather:
+        if 0 <= s - 3 < n_early:
             ag(s - 3, 7).wait_recv()
+        k = s - 2
+        if n_early <= k < n_gather:
+            for m in (0, 1, 2):
+                ag(k, m).wait_recv()
+            ag(k, 7).start()
+        if n_early <= k - 1 < n_gather:
+            ag(k - 1, 7).wait_recv()
+
+    steps = [0]
+
+    def tok_piece(i):
+        blk = pl.ds(i * (rows // TOKEN_PIECES), rows // TOKEN_PIECES)
+        return remote(tok_hbm.at[blk, :], xp.at[blk, :], extra_s.at[1 + i], extra_r.at[1 + i], y_peer)
+
+    def tok_send(i):
+        @pl.when(first)
+        def _():
+            tok_piece(i).start()
+
+    def ag_until(at, more=0):
+        goal = max(p.held(at), steps[0] + more - 1)
+        while steps[0] <= goal:
+            ag_step(steps[0])
+            for i in range(TOKEN_PIECES):
+                if i // TOKENS_A_STEP == steps[0]:
+                    tok_send(i)
+            steps[0] += 1
+            if steps[0] == 1:
+                ag_late_turn()
+            if steps[0] == 5:
+                ag_late_z()
+
+    def ag_late_turn():
+        for k in sorted(p.gather_late):
+            ag(k, 3).wait_recv()
+            ag(k, 5).start()
+            ag(k, 4).wait_recv()
+            ag(k, 6).start()
+
+    def ag_late_z():
+        for k in sorted(p.gather_late):
+            ag(k, 5).wait_recv()
+            ag(k, 6).wait_recv()
+            for m in (0, 1, 2):
+                ag(k, m).start()
 
     load_tok = pltpu.make_async_copy(tok_hbm, TB, loc.at[0])
     load_tok.start()
-    own_w = pltpu.make_async_copy(shard_ref, W.at[y, z, x, c], loc.at[1])
-    own_w.start()
+    packing = []
+    for src, at, size in (
+        (k_hbm, p.k_at, hc), (v_hbm, p.v_at, hc), (q_hbm, p.q_at, hc), (o_hbm, p.o_at, hc), (d_hbm, p.d_at, ff)
+    ):
+        packing.append((src, own_w.at[:, pl.ds(at, size)]))
+    for t in range(ff // LANES):
+        for n, src in enumerate((g_hbm, u_hbm)):
+            to = own_w.at[:, pl.ds(p.gu_at + (2 * t + n) * LANES, LANES)]
+            packing.append((src.at[:, pl.ds(t * LANES, LANES)], to))
+    packing = [pltpu.make_async_copy(src, to, pack_sem.at[i]) for i, (src, to) in enumerate(packing)]
+    for copy in packing:
+        copy.start()
     barrier = pltpu.get_barrier_semaphore()
     for peer in [core_peer, x_peer, y_peer] + z_peers:
         pl.semaphore_signal(barrier, inc=1, device_id=peer, device_id_type=MESH)
+    count = gain_shard.shape[0]
+    spread = jnp.concatenate([gain_shard[...], jnp.zeros((LANES - count, p.shard_rows), f32)], axis=0)
+    W[y, z, x, c, :, pl.ds(0, LANES)] = jnp.transpose(spread).astype(bf16)
+    for copy in packing:
+        copy.wait()
     pl.semaphore_wait(barrier, 6)
 
-    tok_send = remote(tok_hbm, xp, extra_s.at[0], extra_r.at[0], y_peer)
-
-    @pl.when(first)
-    def _():
-        tok_send.start()
-
-    for k in range(n_gather):
+    for k in sorted(p.gather_late):
+        ag(k, 3).start()
+        ag(k, 4).start()
+
+    for k in range(n_early):
         for m in (0, 1, 2):
             ag(k, m).start()
-    own_w.wait()
     load_tok.wait()
+
+    def tables(i):
+        blk = pl.ds(pl.multiple_of(i * 64, 64), 64)
+        place = (lax.broadcasted_iota(jnp.int32, (64, LANES), 0) + i * 64).astype(f32)
+        angle = place * inverse_ref[...]
+        cos_ref[blk, :] = jnp.cos(angle)
+        turned = jnp.sin(angle)
+        sin_ref[blk, :] = jnp.where(lax.broadcasted_iota(jnp.int32, (64, LANES), 1) < HALF, -turned, turned)
+
+    loop(2 * rows // 64, tables)
 
     start = starts_ref[0, y] - y * rows
 
@@ -577,9 +692,7 @@
     build_mask(0)
     dgains[...] = jnp.zeros_like(dgains)
 
-    for s in range(0, 4):
-        ag_step(s)
-
+    ag_until(LANES)
     gains[0:8, 0:width] = jnp.transpose(weight(0, 0, LANES).astype(f32))[0:8, :]
 
     def norm_in(src, dst):
@@ -590,14 +703,6 @@
         by_rows(body)
 
     norm_in(TB, xo)
-
-    @pl.when(second)
-    def _():
-        tok_send.wait_recv()
-        norm_in(xp, xp)
-
-    ag_step(4)
-    ag_step(5)
 
     def rotated(u, place, sign):
         return u * cos_ref[place, :] + sign * (pltpu.roll(u, HALF, 1) * sin_ref[place, :])
@@ -616,16 +721,31 @@
 
     own_place = pl.ds(pl.multiple_of(y * rows, rows), rows)
     old_place = pl.ds(0, rows)
+    ag_until(p.v_at)
     project(xo, KVQ, 0, own_place, True)
+    ag_until(p.q_at)
     project(xo, KVQ, hc, own_place, False)
+
+    @pl.when(second)
+    def _():
+        for i in range(TOKEN_PIECES):
+            tok_piece(i).wait_recv()
+        norm_in(xp, xp)
+
+    ag_until(p.o_at)
     project(xo, KVQ, 2 * hc, own_place, True)
 
     @pl.when(second)
     def _():
         project(xp, KVp, 0, old_place, True)
+
+    ag_until(p.gu_at)
+
+    @pl.when(second)
+    def _():
         project(xp, KVp, hc, old_place, False)
 
-    ag_step(6)
+    ag_until(0, 1)
 
     per_y = hc // HEAD_DIM
     attn_scale = 1.0 / math.sqrt(HEAD_DIM)
@@ -670,8 +790,10 @@
             loop(2 * (hi - lo), lambda i: attend(i + 2 * lo, True))
 
     stat_a[...] = jnp.zeros_like(stat_a)
-    attend_heads(0, p.heads)
-    ag_step(7)
+    for h in range(0, p.heads, 2):
+        attend_heads(h, h + 2)
+        ag_until(0, 1)
+
 
     def o_proj(zz):
         cols = pl.ds(pl.multiple_of(zz * (width // 4), width // 4), width // 4)
@@ -690,7 +812,6 @@
     by_rows(mid_rows)
     load_og = pltpu.make_async_copy(og_hbm, TB, loc.at[0])
     load_og.start()
-    ag_step(8)
 
     def gate_up(lo, hi):
         def run(i):
@@ -706,20 +827,29 @@
 
         loop(2 * (hi - lo), run)
 
-    ag_step(9)
-    gate_up(0, 6)
-    ag_step(10)
-    ag_step(11)
-    ag_step(12)
-    gate_up(6, 2 * ff // 256)
-    for s in range(13, n_gather + 3):
-        ag_step(s)
-
-    def down_proj(zz):
-        cols = pl.ds(pl.multiple_of(zz * (width // 4), width // 4), width // 4)
-        bff[:, cols] = dot_nt(HID[0], weight(0, p.d_at, ff, zz)) + dot_nt(HID[1], weight(1, p.d_at, ff, zz))
-
-    loop(4, down_proj)
+    ag_until(0, 1)
+    tiles = 2 * ff // 256
+    for lo in range(0, tiles, 4):
+        hi = min(lo + 4, tiles)
+        ag_until(p.gu_at + hi * 256)
+        gate_up(lo, hi)
+        ag_until(0, 1)
+
+    def down_proj(lo, hi, more):
+        def run(zz):
+            cols = pl.ds(pl.multiple_of(zz * (width // 4), width // 4), width // 4)
+            acc = dot_nt(HID[0, :, lo:hi], weight(0, p.d_at + lo, hi - lo, zz)) + dot_nt(
+                HID[1, :, lo:hi], weight(1, p.d_at + lo, hi - lo, zz)
+            )
+            bff[:, cols] = bff[:, cols] + acc if more else acc
+
+        loop(4, run)
+
+    early = ff - sum(size for k, (at, size) in enumerate(p.gather) if k in p.gather_late)
+    ag_until(p.d_at + early)
+    down_proj(0, early, False)
+    ag_until(p.cols)
+    down_proj(early, ff, True)
     load_og.wait()
 
     def out_rows(blk):
@@ -740,55 +870,132 @@
 
     n_reduce = len(p.reduce)
 
+    def rs_parts(j):
+        at, size = p.reduce[j]
+        half = size // 2 // LANES * LANES
+        return (pl.ds(at, half), pl.ds(0, half)), (pl.ds(at + half, size - half), pl.ds(half, size - half))
+
     def rs(j, m):
         at, size = p.reduce[j]
         cols, slot, part = pl.ds(at, size), j % 2, pl.ds(0, size)
         sem = (rs_s.at[j, m], rs_r.at[j, m])
-        low, high = pl.ds(0, 2), pl.ds(2, 2)
         if m == 0:
             return remote(W.at[:, :, :, 1 - c, :, cols], R1.at[slot, :, :, :, :, part], *sem, core_peer)
+        d = m - 5
+        if j in p.reduce_late:
+            (cols_a, part_a), (cols_b, part_b) = rs_parts(j)
+            if m == 1:
+                return remote(W.at[1 - y, z, :, c, :, cols_a], RQ2.at[j, :, :, part_a], *sem, y_peer)
+            if m == 2:
+                return remote(W.at[:, z, 1 - x, c, :, cols_b], RQ2.at[j, :, :, part_b], *sem, x_peer)
+            if m == 3:
+                return remote(W.at[y, z, 1 - x, c, :, cols_a], RQ3.at[j, :, part_a], *sem, x_peer)
+            if m == 4:
+                return remote(W.at[1 - y, z, x, c, :, cols_b], RQ3.at[j, :, part_b], *sem, y_peer)
+            return remote(W.at[:, up(d + 1), :, c, :, cols], RQ1.at[j, d, :, :, :, part], *sem, z_peers[d])
+        low, high = pl.ds(0, p.split_sum(j)), pl.ds(p.split_sum(j), 4 - p.split_sum(j))
         if m == 1:
-            return remote(W.at[1 - y, low, :, c, :, cols], R2A.at[slot, :, :, :, part], *sem, y_peer)
+            return remote(W.at[1 - y, low, :, c, :, cols], R2A.at[slot, low, :, :, part], *sem, y_peer)
         if m == 2:
-            return remote(W.at[:, high, 1 - x, c, :, cols], R2B.at[slot, :, :, :, part], *sem, x_peer)
+            return remote(W.at[:, high, 1 - x, c, :, cols], R2B.at[slot, :, pl.ds(0, 4 - p.split_sum(j)), :, part], *sem, x_peer)
         if m == 3:
-            return remote(W.at[y, low, 1 - x, c, :, cols], R3A.at[slot, :, :, part], *sem, x_peer)
+            return remote(W.at[y, low, 1 - x, c, :, cols], R3A.at[slot, low, :, part], *sem, x_peer)
         if m == 4:
-            return remote(W.at[1 - y, high, x, c, :, cols], R3B.at[slot, :, :, part], *sem, y_peer)
-        d = m - 5
+            return remote(W.at[1 - y, high, x, c, :, cols], R3B.at[slot, pl.ds(0, 4 - p.split_sum(j)), :, part], *sem, y_peer)
         return remote(W.at[y, up(d + 1), x, c, :, cols], R4.at[slot, d, :, part], *sem, z_peers[d])
 
     rs_sources = [core_peer, y_peer, x_peer, x_peer, y_peer] + z_sources
+    n_late = len(p.reduce_late)
+
+    def rs_first(m):
+        return 2 if m == 0 else n_late + 2
 
     def rs_start(j, m):
-        if j >= 2:
+        if j >= rs_first(m):
             pl.semaphore_wait(credit.at[m], 1)
         rs(j, m).start()
 
     def rs_used(j, m):
-        if j + 2 < n_reduce:
+        if j + 2 < n_reduce and j + 2 >= rs_first(m):
             pl.semaphore_signal(credit.at[m], inc=1, device_id=rs_sources[m], device_id_type=MESH)
 
-    def put_sum(j):
-        at, size = p.reduce[j]
+    finished = []
+
+    def put_sum(i):
+        at, size = p.reduce[finished[i]]
         return pltpu.make_async_copy(
-            ST.at[j % 2, :, pl.ds(0, size)], gr_hbm.at[:, pl.ds(at, size)], loc.at[2 + j % 2]
+            ST.at[i % 2, :, pl.ds(0, size)], gr_hbm.at[:, pl.ds(at, size)], loc.at[2 + i % 2]
         )
 
-    def rs_event(j, phase):
+    def finish(j, total):
+        i = len(finished)
+        finished.append(j)
+        if i >= 2:
+            put_sum(i - 2).wait()
+        ST[i % 2, :, pl.ds(0, p.reduce[j][1])] = total
+        put_sum(i).start()
+
+    def rs_core(j):
         at, size = p.reduce[j]
         cols, slot, part = pl.ds(at, size), j % 2, pl.ds(0, size)
+        rs(j, 0).wait_recv()
+
+        def add(i):
+            a, b, d = i // 8, lax.rem(i // 2, 4), lax.rem(i, 2)
+            W[a, b, d, c, :, cols] = W[a, b, d, c, :, cols] + R1[slot, a, b, d, :, part]
+
+        loop(16, add)
+        rs_used(j, 0)
+
+    def rs_late_event(j, phase):
+        at, size = p.reduce[j]
+        cols, part = pl.ds(at, size), pl.ds(0, size)
+        (cols_a, part_a), (cols_b, part_b) = rs_parts(j)
         if phase == 0:
             rs_start(j, 0)
         elif phase == 1:
-            rs(j, 0).wait_recv()
-
-            def add(i):
-                a, b, d = i // 8, lax.rem(i // 2, 4), lax.rem(i, 2)
-                W[a, b, d, c, :, cols] = W[a, b, d, c, :, cols] + R1[slot, a, b, d, :, part]
-
-            loop(16, add)
-            rs_used(j, 0)
+            rs_core(j)
+            for m in (5, 6, 7):
+                rs_start(j, m)
+        elif phase == 2:
+            for m in (5, 6, 7):
+                rs(j, m).wait_recv()
+
+            def add_q(i):
+                a, b = i // 2, lax.rem(i, 2)
+                total = W[a, z, b, c, :, cols].astype(f32)
+                for d in range(3):
+                    total = total + RQ1[j, d, a, b, :, part].astype(f32)
+                W[a, z, b, c, :, cols] = total.astype(bf16)
+
+            loop(4, add_q)
+            rs_start(j, 1)
+            rs_start(j, 2)
+        elif phase == 3:
+            rs(j, 1).wait_recv()
+            rs(j, 2).wait_recv()
+            for d in range(2):
+                W[y, z, d, c, :, cols_a] = W[y, z, d, c, :, cols_a] + RQ2[j, d, :, part_a]
+                W[d, z, x, c, :, cols_b] = W[d, z, x, c, :, cols_b] + RQ2[j, d, :, part_b]
+            rs_start(j, 3)
+            rs_start(j, 4)
+        else:
+            rs(j, 3).wait_recv()
+            rs(j, 4).wait_recv()
+            finish(j, W[y, z, x, c, :, cols].astype(f32) + RQ3[j, :, part].astype(f32))
+
+    def rs_event(j, phase):
+        if j in p.reduce_late:
+            rs_late_event(j, phase)
+            return
+        at, size = p.reduce[j]
+        cols, slot, part = pl.ds(at, size), j % 2, pl.ds(0, size)
+        n_low = p.split_sum(j)
+        n_high = 4 - n_low
+        if phase == 0:
+            rs_start(j, 0)
+        elif phase == 1:
+            rs_core(j)
             rs_start(j, 1)
             rs_start(j, 2)
         elif phase == 2:
@@ -798,48 +1005,51 @@
                 b, d = i // 2, lax.rem(i, 2)
                 W[y, b, d, c, :, cols] = W[y, b, d, c, :, cols] + R2A[slot, b, d, :, part]
 
-            loop(4, add_a)
+            loop(2 * n_low, add_a)
             rs_used(j, 1)
             rs_start(j, 3)
             rs(j, 2).wait_recv()
 
             def add_b(i):
-                a, b = i // 2, lax.rem(i, 2)
-                W[a, b + 2, x, c, :, cols] = W[a, b + 2, x, c, :, cols] + R2B[slot, a, b, :, part]
-
-            loop(4, add_b)
+                a, b = i // n_high, lax.rem(i, n_high)
+                W[a, b + n_low, x, c, :, cols] = W[a, b + n_low, x, c, :, cols] + R2B[slot, a, b, :, part]
+
+            loop(2 * n_high, add_b)
             rs_used(j, 2)
             rs_start(j, 4)
         elif phase == 3:
             rs(j, 3).wait_recv()
+            for b in range(n_low):
+                W[y, b, x, c, :, cols] = W[y, b, x, c, :, cols] + R3A[slot, b, :, part]
+            rs_used(j, 3)
             rs(j, 4).wait_recv()
-            for b in range(2):
-                W[y, b, x, c, :, cols] = W[y, b, x, c, :, cols] + R3A[slot, b, :, part]
-                W[y, b + 2, x, c, :, cols] = W[y, b + 2, x, c, :, cols] + R3B[slot, b, :, part]
-            rs_used(j, 3)
+            for b in range(n_high):
+                W[y, b + n_low, x, c, :, cols] = W[y, b + n_low, x, c, :, cols] + R3B[slot, b, :, part]
             rs_used(j, 4)
             for m in (5, 6, 7):
                 rs_start(j, m)
         else:
             for m in (5, 6, 7):
                 rs(j, m).wait_recv()
-            if j >= 2:
-                put_sum(j - 2).wait()
             total = W[y, z, x, c, :, cols].astype(f32)
             for d in range(3):
                 total = total + R4[slot, d, :, part].astype(f32)
-            ST[slot, :, part] = total
             for m in (5, 6, 7):
                 rs_used(j, m)
-            put_sum(j).start()
-
-    events = [(j, t - j) for t in range(n_reduce + 4) for j in range(n_reduce) if 0 <= t - j <= 4]
+            finish(j, total)
+
+    def slot_of(j, phase):
+        return j + (LATE_SLOTS[phase] if j in p.reduce_late else phase)
+
+    events = sorted(
+        ((j, phase) for j in range(n_reduce) for phase in range(5)), key=lambda e: (slot_of(*e), -e[0], e[1])
+    )
     done = [0]
 
     def pump(ready, until):
         while done[0] < len(events):
             j, phase = events[done[0]]
-            if j >= ready or j + phase >= until:
+            if j >= ready or slot_of(j, phase) >= until:
                 break
             rs_event(j, phase)
             done[0] += 1
@@ -854,36 +1064,43 @@
 
     pairs = ff // 256
 
-    def back_pair(i):
-        yy, t = i // pairs, lax.rem(i, pairs)
-        bh = dot_nn(BF[...], weight(yy, p.d_at + pl.multiple_of(t * 256, 256), 256))
-        back_tile(yy, 2 * t, bh[:, 0:LANES])
-        back_tile(yy, 2 * t + 1, bh[:, LANES:256])
-
-    def back_last(yy):
+    def back_hidden(lo, hi):
+        def run(i):
+            yy, t = i // (hi - lo), lax.rem(i, hi - lo) + lo
+            bh = dot_nn(BF[...], weight(yy, p.d_at + pl.multiple_of(t * 256, 256), 256))
+            back_tile(yy, 2 * t, bh[:, 0:LANES])
+            back_tile(yy, 2 * t + 1, bh[:, LANES:256])
+
+        loop(2 * (hi - lo), run)
+
+    def grad_down(lo, hi):
+        def run(i):
+            yy, off = i // (hi - lo), pl.multiple_of((lax.rem(i, hi - lo) + lo) * 256, 256)
+            put_weight(yy, p.d_at + off, 256, dot_nn(T[...], HID[yy, :, pl.ds(off, 256)]))
+
+        loop(2 * (hi - lo), run)
+
+    def back_hidden_last(yy):
         bh = dot_nn(BF[...], weight(yy, p.d_at + pairs * 256, LANES))
         back_tile(yy, jnp.int32(2 * pairs), bh)
 
-    loop(2 * pairs, back_pair)
-    if ff % 256:
-        loop(2, back_last)
-
-    T[...] = jnp.transpose(BF[...])
-
-    def grad_down_pair(i):
-        yy, off = i // pairs, pl.multiple_of(lax.rem(i, pairs) * 256, 256)
-        put_weight(yy, p.d_at + off, 256, dot_nn(T[...], HID[yy, :, pl.ds(off, 256)]))
-
     def grad_down_last(yy):
         put_weight(yy, p.d_at + pairs * 256, LANES, dot_nn(T[...], HID[yy, :, pl.ds(pairs * 256, LANES)]))
 
-    loop(2 * pairs, grad_down_pair)
+    n_d = len(p.d_cuts)
+    n_gu = n_d + len(p.gu_cuts)
+    first_pairs = p.d_cuts[0][1] // 256
+    T[...] = jnp.transpose(BF[...])
+    back_hidden(0, first_pairs)
+    grad_down(0, first_pairs)
+    pump(1, PACE[0])
+    back_hidden(first_pairs, pairs)
+    if ff % 256:
+        loop(2, back_hidden_last)
+    grad_down(first_pairs, pairs)
     if ff % 256:
         loop(2, grad_down_last)
-
-    n_d = len(p.d_cuts)
-    n_gu = n_d + len(p.gu_cuts)
-    pump(n_d, 2)
+    pump(n_d, PACE[1])
 
     def back_normed(zz):
         cols = pl.ds(pl.multiple_of(zz * (width // 4), width // 4), width // 4)
@@ -892,8 +1109,10 @@
         acc = acc + dot_nt(GU[1, :, 0:ff], weight(1, p.gu_at, ff, zz))
         bff[:, cols] = acc + dot_nt(GU[1, :, ff : 2 * ff], weight(1, p.gu_at + ff, ff, zz))
 
-    loop(4, back_normed)
-    pump(n_d, 4)
+    loop(2, back_normed)
+    pump(n_d, PACE[1] + 1)
+    loop(2, lambda i: back_normed(i + 2))
+    pump(n_d, PACE[2])
     T[...] = jnp.transpose(nf[...])
 
     def grad_gate_up(lo, hi):
@@ -904,9 +1123,9 @@
         loop(2 * (hi - lo), run)
 
     grad_gate_up(0, 4)
-    pump(n_d + 2, 5)
+    pump(n_d + 2, PACE[3])
     grad_gate_up(4, 2 * ff // 256)
-    pump(n_gu, 6)
+    pump(n_gu, PACE[4])
 
     def mid_back(blk):
         m = mid[blk, :]
@@ -923,7 +1142,7 @@
     by_rows(mid_back)
     load_again = pltpu.make_async_copy(tok_hbm, TB, loc.at[0])
     load_again.start()
-    pump(n_gu, 7)
+    pump(n_gu, PACE[5])
 
     per_o = hc // 256
 
@@ -939,7 +1158,7 @@
         put_weight(yy, p.o_at + off, 256, dot_nn(T[...], att[:, cut(yy * hc + off, 256)]))
 
     loop(2 * per_o, grad_out_tile)
-    pump(n_gu + 1, 8)
+    pump(n_gu + 1, PACE[6])
 
     stat_b[...] = jnp.zeros_like(stat_b)
     for h in range(p.heads):
@@ -952,7 +1171,7 @@
     gains[8 : 8 + p.heads, rows : 2 * rows] = inner_rows
     build_mask(1)
 
-    def attend_grad(h, both):
+    def attend_grad(h):
         yy, k_at, v_at, q_at = head_at(h)
         q = KVQ[yy, :, q_at]
         do = nf[:, pl.ds(pl.multiple_of(h * HEAD_DIM, HEAD_DIM), HEAD_DIM)]
@@ -973,28 +1192,24 @@
             ref[yy, :, k_at] = rotated(dk, place, -1.0).astype(bf16)
             return dq
 
-        dq = side(KVQ, own_place, True)
-        if both:
-            dq = dq + side(KVp, old_place, False)
-        KVQ[yy, :, q_at] = rotated(dq, own_place, -1.0).astype(bf16)
-
-    def grad_heads(lo, hi):
-        @pl.when(first)
-        def _():
-            loop(hi - lo, lambda h: attend_grad(h + lo, False))
+        DQ[...] = side(KVQ, own_place, True)
 
         @pl.when(second)
         def _():
-            loop(hi - lo, lambda h: attend_grad(h + lo, True))
-
-    half_heads = p.heads // 2
-    grad_heads(0, half_heads)
-    pump(n_gu + 1, 10)
-    grad_heads(half_heads, p.heads)
-    pump(n_gu + 1, 11)
+            DQ[...] += side(KVp, old_place, False)
+
+        KVQ[yy, :, q_at] = rotated(DQ[...], own_place, -1.0).astype(bf16)
+
+    def grad_heads(lo, hi):
+        loop(hi - lo, lambda h: attend_grad(h + lo))
+
+    for i in range(4):
+        grad_heads(i * p.heads // 4, (i + 1) * p.heads // 4)
+        pump(n_gu + 1, PACE[7 + i])
+
     put_out.wait()
 
-    back_send = remote(LO, KVp.at[0, :, pl.ds(0, width)], extra_s.at[1], extra_r.at[1], y_peer)
+    back_send = remote(LO, KVp.at[0, :, pl.ds(0, width)], extra_s.at[0], extra_r.at[0], y_peer)
 
     @pl.when(second)
     def _():
@@ -1012,7 +1227,7 @@
         bff[:, cols] = dot_nt(KVQ[0], weight(0, p.k_at, p.kvq, zz)) + dot_nt(KVQ[1], weight(1, p.k_at, p.kvq, zz))
 
     loop(4, own_back)
-    pump(n_gu + 1, 12)
+    pump(n_gu + 1, PACE[11])
     T[...] = jnp.transpose(xo[...])
     tiles = p.kvq // 256
 
@@ -1036,7 +1251,7 @@
 
         loop(2 * old_tiles, grad_old)
 
-    pump(n_reduce - 1, 13)
+    pump(n_reduce - 1, PACE[12])
     load_again.wait()
 
     @pl.when(first)
@@ -1062,10 +1277,10 @@
     gain_cols = jnp.transpose(jnp.concatenate([dgains[...], jnp.zeros((LANES - 8, width), f32)], axis=0))
     put_weight(0, 0, LANES, gain_cols)
     put_weight(1, 0, LANES, gain_cols)
-    pump(n_reduce, len(events))
+    pump(n_reduce, len(events) * 2)
     put_ig.wait()
-    for j in (n_reduce - 2, n_reduce - 1):
-        put_sum(j).wait()
+    for i in (n_reduce - 2, n_reduce - 1):
+        put_sum(i).wait()
 
     for j in range(n_reduce):
         for m in range(8):
@@ -1073,44 +1288,43 @@
 
     @pl.when(first)
     def _():
-        tok_send.wait_send()
+        for i in range(TOKEN_PIECES):
+            tok_piece(i).wait_send()
 
     @pl.when(second)
     def _():
         back_send.wait_send()
 
 
-def pack_rows(plan, weights, gain_shards):
-    query, key, value, out, gate, up, down = weights
-    shard_rows = plan.shard_rows
-    columns = jnp.stack(gain_shards, axis=1)
-    columns = jnp.pad(columns, ((0, 0), (0, LANES - columns.shape[1])))
-    turns = jnp.stack(
-        [gate.reshape(shard_rows, -1, LANES), up.reshape(shard_rows, -1, LANES)], axis=2
-    ).reshape(shard_rows, -1)
-    return jnp.concatenate([columns, key, value, query, out.T, turns, down.T], axis=1)
-
-
-def unpack_rows(plan, total):
+def finish_layer(plan, out_hbm, ig_hbm, total, out_to, ig_to, gq, gk, gv, go, gg, gu, gd, g0, g1, g2, g3, o_buf, i_buf, sems):
     hc, ff = plan.head_cols, plan.ff_cols
-
-    def piece(at, size):
-        return total[:, at : at + size]
-
-    turns = piece(plan.gu_at, 2 * ff).reshape(plan.shard_rows, -1, 2, LANES)
-    return (
-        piece(plan.q_at, hc),
-        piece(plan.k_at, hc),
-        piece(plan.v_at, hc),
-        piece(plan.o_at, hc).T,
-        turns[:, :, 0].reshape(plan.shard_rows, ff),
-        turns[:, :, 1].reshape(plan.shard_rows, ff),
-        piece(plan.d_at, ff).T,
-        total[:, 0],
-        total[:, 1],
-        total[:, 2],
-        total[:, 3],
-    )
+    loads = (
+        pltpu.make_async_copy(out_hbm, o_buf, sems.at[0]),
+        pltpu.make_async_copy(ig_hbm, i_buf, sems.at[1]),
+    )
+    stores = (
+        pltpu.make_async_copy(o_buf, out_to, sems.at[2]),
+        pltpu.make_async_copy(i_buf, ig_to, sems.at[3]),
+    )
+    for copy in loads:
+        copy.start()
+    gq[...] = total[:, plan.q_at : plan.q_at + hc]
+    gk[...] = total[:, plan.k_at : plan.k_at + hc]
+    gv[...] = total[:, plan.v_at : plan.v_at + hc]
+    go[...] = total[:, plan.o_at : plan.o_at + hc]
+    for load, store in zip(loads, stores):
+        load.wait()
+        store.start()
+    gd[...] = total[:, plan.d_at : plan.d_at + ff]
+    for t in range(ff // LANES):
+        at = plan.gu_at + 2 * t * LANES
+        gg[:, t * LANES : (t + 1) * LANES] = total[:, at : at + LANES]
+        gu[:, t * LANES : (t + 1) * LANES] = total[:, at + LANES : at + 2 * LANES]
+    gains = jnp.transpose(total[:, 0:LANES])
+    for i, ref in enumerate((g0, g1, g2, g3)):
+        ref[...] = gains[i : i + 1, :]
+    for store in stores:
+        store.wait()
 
 
 def fused_on_device(
@@ -1131,15 +1345,9 @@
 ):
     rows, width = tokens.shape
     plan = Plan(rows, width, query_weight.shape[1], gate_weight.shape[1], query_weight.shape[0])
-    shard = pack_rows(
-        plan,
-        (query_weight, key_weight, value_weight, out_weight, gate_weight, up_weight, down_weight),
-        (gain_attn_in, gain_attn_out, gain_ff_in, gain_ff_out),
-    )
-    cosine, sine = rope_at(jnp.arange(2 * rows, dtype=jnp.int32))
-    cosine, sine = cosine[:, 0], sine[:, 0]
-    cos_table = jnp.concatenate([cosine, cosine], axis=1)
-    sin_table = jnp.concatenate([-sine, sine], axis=1)
+    gain_shard = jnp.stack([gain_attn_in, gain_attn_out, gain_ff_in, gain_ff_out]).astype(f32)
+    half = rope_base ** (-(np.arange(HALF, dtype=np.float32) * 2.0) / HEAD_DIM)
+    inverse = jnp.asarray(np.concatenate([half, half])[None].astype(np.float32))
     hc, ff, sr = plan.head_cols, plan.ff_cols, plan.shard_rows
     anywhere = pl.BlockSpec(memory_space=pl.ANY)
     in_vmem = pl.BlockSpec(memory_space=pltpu.VMEM)
@@ -1166,20 +1374,27 @@
         pltpu.VMEM((8, width), f32),
         pltpu.VMEM((rows, LANES), f32),
         pltpu.VMEM((rows, LANES), f32),
+        pltpu.VMEM((rows, HEAD_DIM), f32),
+        pltpu.VMEM((2 * rows, LANES), f32),
+        pltpu.VMEM((2 * rows, LANES), f32),
         pltpu.VMEM((2, 2, 4, 2, sr, 512), bf16),
         pltpu.VMEM((2, 2, 2, sr, 512), bf16),
-        pltpu.VMEM((2, 2, 2, sr, 512), bf16),
-        pltpu.VMEM((2, 2, sr, 512), bf16),
+        pltpu.VMEM((2, 2, 3, sr, 512), bf16),
         pltpu.VMEM((2, 2, sr, 512), bf16),
         pltpu.VMEM((2, 3, sr, 512), bf16),
+        pltpu.VMEM((2, 3, sr, 512), bf16),
+        pltpu.VMEM((max(1, REDUCE_LATE), 3, 2, 2, sr, 512), bf16),
+        pltpu.VMEM((max(1, REDUCE_LATE), 2, sr, 512), bf16),
+        pltpu.VMEM((max(1, REDUCE_LATE), sr, 512), bf16),
         pltpu.VMEM((2, sr, 512), f32),
         pltpu.SemaphoreType.DMA((n_gather, 8)),
         pltpu.SemaphoreType.DMA((n_gather, 8)),
         pltpu.SemaphoreType.DMA((n_reduce, 8)),
         pltpu.SemaphoreType.DMA((n_reduce, 8)),
         pltpu.SemaphoreType.DMA((4,)),
-        pltpu.SemaphoreType.DMA((2,)),
-        pltpu.SemaphoreType.DMA((2,)),
+        pltpu.SemaphoreType.DMA((5 + 2 * (ff // LANES),)),
+        pltpu.SemaphoreType.DMA((1 + TOKEN_PIECES,)),
+        pltpu.SemaphoreType.DMA((1 + TOKEN_PIECES,)),
         pltpu.SemaphoreType.REGULAR((8,)),
     ]
     out, input_grad, total = pl.pallas_call(
@@ -1189,15 +1404,47 @@
             jax.ShapeDtypeStruct((rows, width), f32),
             jax.ShapeDtypeStruct((sr, plan.cols), f32),
         ),
-        in_specs=[anywhere, anywhere, anywhere, pl.BlockSpec(memory_space=pltpu.SMEM), in_vmem, in_vmem],
+        in_specs=[anywhere] * 7 + [in_vmem] + [anywhere] * 2 + [pl.BlockSpec(memory_space=pltpu.SMEM), in_vmem],
         out_specs=(anywhere, anywhere, anywhere),
         scratch_shapes=scratch,
         compiler_params=pltpu.CompilerParams(
             collective_id=0, has_side_effects=True, vmem_limit_bytes=67043328
         ),
         name="fused_layer",
-    )(shard, tokens, out_grad, piece_starts, cos_table, sin_table)
-    return (out, input_grad) + unpack_rows(plan, total)
+    )(
+        key_weight, value_weight, query_weight, gate_weight, up_weight, out_weight.T, down_weight.T,
+        gain_shard, tokens, out_grad, piece_starts, inverse,
+    )
+
+    def grad(*shape):
+        return jax.ShapeDtypeStruct(shape, f32)
+
+    outs = pl.pallas_call(
+        functools.partial(finish_layer, plan),
+        out_shape=(
+            jax.ShapeDtypeStruct((rows, width), bf16),
+            grad(rows, width),
+            grad(sr, hc),
+            grad(sr, hc),
+            grad(sr, hc),
+            grad(sr, hc),
+            grad(sr, ff),
+            grad(sr, ff),
+            grad(sr, ff),
+        )
+        + (grad(1, sr),) * 4,
+        in_specs=[anywhere, anywhere, in_vmem],
+        out_specs=(anywhere, anywhere) + (in_vmem,) * 11,
+        scratch_shapes=[
+            pltpu.VMEM((rows, width), bf16),
+            pltpu.VMEM((rows, width), f32),
+            pltpu.SemaphoreType.DMA((4,)),
+        ],
+        name="finish_layer",
+    )(out, input_grad, total)
+    outs = list(outs)
+    outs[5], outs[8] = outs[5].T, outs[8].T
+    return tuple(outs[:9]) + tuple(o[0] for o in outs[9:])
 
 
 def fits_fused(mesh, tokens, query_weight, gate_weight, piece_starts):

time: 346 us -> 310 us (0.90)
  local copies, waits for them, and re-layouts: 20.2 us -> 0 us
  Pallas kernels: 321 us -> 308 us
    pallas_call x1, Pallas kernels: 321 us -> 302 us  [fused_on_device(): pl.pallas_call(functools.partial(fused_layer, plan), out_shape=(jax.Shape...]
    unnamed x24 -> x0, local copies, waits for them, and re-layouts: 7.93 us -> none
    pallas_call x0 -> x1, Pallas kernels: none -> 5.86 us  [fused_on_device(): pl.pallas_call(functools.partial(finish_layer, plan), out_shape=(jax.Shap...]
    slice x3 -> x0, local copies, waits for them, and re-layouts: 4.79 us -> none  [the longest x1 1.94 us: unpack_rows(): turns[:, :, 1].reshape(plan.shard_rows, ff)]
    transpose x2 -> x0, local copies, waits for them, and re-layouts: 3.63 us -> none  [the longest x1 1.89 us: unpack_rows(): piece(plan.o_at, hc)]
where the time goes in v2:
time: 310 us
  Pallas kernels  308 us (99%)
    pallas_call x1, Pallas kernels, fused_on_device(): pl.pallas_call(functools.partial(fused_layer, plan), out_shape=(jax.Shape...  302 us

profile of v2, /device:TPU:0, one launch (start us, length us, event | category | flops | bytes accessed | tf_op | source)
XLA Modules:
  0.0 310.0 jit_solution(1006606307562300294)
XLA Ops:
  0.6 1.3 maximum_convert_fusion.gain_shard
  1.9 302.0 %fused_layer.1 = (bf16[512,1024]{1,0:T(8,128)(2,1)}, f32[512,1024]{1,0:T(8,128)}, f32[64,6400]{1,0:T(8,128)}) custom-call(bf16[64,512]{1,0:T(8,128)(2,1)} %k_hbm.1, bf16[64,512]{1,0:T(8,128)(2,1)} %v_hbm.1, bf16[64,512]{1,0:T(8,128)(2,1)} %q_hbm.1, bf16[64,1408]{1,0:T(8,128)(2,1)} %g_hbm.1, bf16[64,1408]{1,0:T(8,128)(2,1)} %u_hbm.1, ...), custom_call_target="tpu_custom_call" | custom-call | tf_op jit(solution)/shard_map/fused_layer/pallas_call | solution.py:1400
  303.9 5.9 %finish_layer.1 = (bf16[512,1024]{1,0:T(8,128)(2,1)}, f32[512,1024]{1,0:T(8,128)}, f32[64,512]{1,0:T(8,128)}, f32[64,512]{1,0:T(8,128)}, f32[64,512]{1,0:T(8,128...) custom-call(bf16[512,1024]{1,0:T(8,128)(2,1)} %get-tuple-element.29., ...), custom_call_target="tpu_custom_call" | custom-call | tf_op jit(solution)/shard_map/finish_layer/pallas_call | solution.py:1422

commit v3 on v2

--- a/solution.py
+++ b/solution.py
@@ -374,17 +374,19 @@
 HALF = HEAD_DIM // 2
 MESH = pl.DeviceIdType.MESH
 GATHER_FIRST = (256, 384)
-GATHER_DOWN = (384, 256, 512, 256)
+GATHER_DOWN = (512, 384, 256, 256)
 REDUCE_DOWN = (512, 512)
 REDUCE_LAST = (256, 256)
 GATHER_LATE = 2
+LATE_STEP = 0
 REDUCE_LATE = 0
 LATE_SLOTS = (0, 1, 6, 7, 8)
 X_FIRST = (1, 2)
 X_FIRST_SUM = (2, 2, 2, 2, 2, 2, 2, 2, 1, 1, 1, 1, 1, 1, 1, 1, 1, 1, 1, 1)
 PACE = (1, 2, 3, 4, 5, 6, 7, 8, 9, 10, 11, 12, 13)
 TOKEN_PIECES = 8
-TOKENS_A_STEP = 2
+TOKENS_EARLY = 4
+TOKENS_A_STEP = 1
 f32 = jnp.float32
 bf16 = jnp.bfloat16
 
@@ -430,11 +432,15 @@
             + cuts(self.k_at, head_cols, REDUCE_LAST)
             + [(0, LANES)]
         )
-        self.gather_late = set(range(len(self.gather) - GATHER_LATE, len(self.gather)))
+        down = len(self.gather) - len(cuts(self.d_at, ff_cols, GATHER_DOWN))
+        self.gather_late = list(range(down, down + GATHER_LATE))
+        self.gather_early = [k for k in range(len(self.gather)) if k not in self.gather_late]
         self.reduce_late = set(range(REDUCE_LATE))
 
     def held(self, at):
-        return next(k for k, (start, size) in enumerate(self.gather) if start + size >= at) + 3
+        early = [i + 3 for i, k in enumerate(self.gather_early) if self.gather[k][0] < at]
+        late = [len(self.gather_early) + LATE_STEP + 1 for k in self.gather_late if self.gather[k][0] < at]
+        return max(early + late + [0])
 
     def split(self, k):
         return X_FIRST[k % len(X_FIRST)]
@@ -568,32 +574,40 @@
         return remote(ref, ref, *sem, core_peer)
 
     n_gather = len(p.gather)
-    n_early = n_gather - len(p.gather_late)
+    n_early = len(p.gather_early)
 
     def ag_step(s):
-        if 0 <= s < n_early:
-            for m in (0, 1, 2):
-                ag(s, m).wait_recv()
-            ag(s, 3).start()
-            ag(s, 4).start()
-        if 0 <= s - 1 < n_early:
-            ag(s - 1, 3).wait_recv()
-            ag(s - 1, 5).start()
-            ag(s - 1, 4).wait_recv()
-            ag(s - 1, 6).start()
-        if 0 <= s - 2 < n_early:
-            ag(s - 2, 5).wait_recv()
-            ag(s - 2, 6).wait_recv()
-            ag(s - 2, 7).start()
-        if 0 <= s - 3 < n_early:
-            ag(s - 3, 7).wait_recv()
-        k = s - 2
-        if n_early <= k < n_gather:
+        def early(i):
+            return p.gather_early[i] if 0 <= i < n_early else None
+
+        k = early(s)
+        if k is not None:
             for m in (0, 1, 2):
                 ag(k, m).wait_recv()
+            ag(k, 3).start()
+            ag(k, 4).start()
+        k = early(s - 1)
+        if k is not None:
+            ag(k, 3).wait_recv()
+            ag(k, 5).start()
+            ag(k, 4).wait_recv()
+            ag(k, 6).start()
+        k = early(s - 2)
+        if k is not None:
+            ag(k, 5).wait_recv()
+            ag(k, 6).wait_recv()
             ag(k, 7).start()
-        if n_early <= k - 1 < n_gather:
-            ag(k - 1, 7).wait_recv()
+        k = early(s - 3)
+        if k is not None:
+            ag(k, 7).wait_recv()
+        if s == n_early + LATE_STEP:
+            for k in p.gather_late:
+                for m in (0, 1, 2):
+                    ag(k, m).wait_recv()
+                ag(k, 7).start()
+        if s == n_early + LATE_STEP + 1:
+            for k in p.gather_late:
+                ag(k, 7).wait_recv()
 
     steps = [0]
 
@@ -610,8 +624,8 @@
         goal = max(p.held(at), steps[0] + more - 1)
         while steps[0] <= goal:
             ag_step(steps[0])
-            for i in range(TOKEN_PIECES):
-                if i // TOKENS_A_STEP == steps[0]:
+            for i in range(TOKENS_EARLY, TOKEN_PIECES):
+                if (i - TOKENS_EARLY) // TOKENS_A_STEP == steps[0]:
                     tok_send(i)
             steps[0] += 1
             if steps[0] == 1:
@@ -620,14 +634,14 @@
                 ag_late_z()
 
     def ag_late_turn():
-        for k in sorted(p.gather_late):
+        for k in p.gather_late:
             ag(k, 3).wait_recv()
             ag(k, 5).start()
             ag(k, 4).wait_recv()
             ag(k, 6).start()
 
     def ag_late_z():
-        for k in sorted(p.gather_late):
+        for k in p.gather_late:
             ag(k, 5).wait_recv()
             ag(k, 6).wait_recv()
             for m in (0, 1, 2):
@@ -657,13 +671,15 @@
         copy.wait()
     pl.semaphore_wait(barrier, 6)
 
-    for k in sorted(p.gather_late):
+    for k in p.gather_late:
         ag(k, 3).start()
         ag(k, 4).start()
 
-    for k in range(n_early):
+    for k in p.gather_early:
         for m in (0, 1, 2):
             ag(k, m).start()
+    for i in range(TOKENS_EARLY):
+        tok_send(i)
     load_tok.wait()
 
     def tables(i):
@@ -829,11 +845,10 @@
 
     ag_until(0, 1)
     tiles = 2 * ff // 256
-    for lo in range(0, tiles, 4):
-        hi = min(lo + 4, tiles)
+    for lo in range(0, tiles, 2):
+        hi = min(lo + 2, tiles)
         ag_until(p.gu_at + hi * 256)
         gate_up(lo, hi)
-        ag_until(0, 1)
 
     def down_proj(lo, hi, more):
         def run(zz):
@@ -845,11 +860,13 @@
 
         loop(4, run)
 
-    early = ff - sum(size for k, (at, size) in enumerate(p.gather) if k in p.gather_late)
-    ag_until(p.d_at + early)
-    down_proj(0, early, False)
-    ag_until(p.cols)
-    down_proj(early, ff, True)
+    ready = 0
+    for n, (at, size) in enumerate(p.gather[p.gather_late[0] :]):
+        if n >= GATHER_LATE - 1:
+            ag_until(at + size)
+            down_proj(ready, at + size - p.d_at, ready > 0)
+            ready = at + size - p.d_at
+
     load_og.wait()
 
     def out_rows(blk):
@@ -1296,30 +1313,38 @@
         back_send.wait_send()
 
 
-def finish_layer(plan, out_hbm, ig_hbm, total, out_to, ig_to, gq, gk, gv, go, gg, gu, gd, g0, g1, g2, g3, o_buf, i_buf, sems):
+def finish_layer(plan, out_hbm, ig_hbm, total_hbm, out_to, ig_to, gq, gk, gv, go, gg, gu, gd, g0, g1, g2, g3, bufs, sems):
+    o_buf, i_buf, total = bufs
+    load_sem, store_sem = sems
     hc, ff = plan.head_cols, plan.ff_cols
-    loads = (
-        pltpu.make_async_copy(out_hbm, o_buf, sems.at[0]),
-        pltpu.make_async_copy(ig_hbm, i_buf, sems.at[1]),
-    )
-    stores = (
-        pltpu.make_async_copy(o_buf, out_to, sems.at[2]),
-        pltpu.make_async_copy(i_buf, ig_to, sems.at[3]),
-    )
-    for copy in loads:
-        copy.start()
-    gq[...] = total[:, plan.q_at : plan.q_at + hc]
-    gk[...] = total[:, plan.k_at : plan.k_at + hc]
-    gv[...] = total[:, plan.v_at : plan.v_at + hc]
-    go[...] = total[:, plan.o_at : plan.o_at + hc]
-    for load, store in zip(loads, stores):
+    cuts = ((0, plan.gu_at), (plan.gu_at, 2 * ff), (plan.d_at, ff))
+    loads = [pltpu.make_async_copy(out_hbm, o_buf, load_sem.at[0]), pltpu.make_async_copy(ig_hbm, i_buf, load_sem.at[1])]
+    for i, (at, size) in enumerate(cuts):
+        cols = pl.ds(at, size)
+        loads.append(pltpu.make_async_copy(total_hbm.at[:, cols], total.at[:, cols], load_sem.at[2 + i]))
+    moves = [[(o_buf, out_to)], [(i_buf, ig_to)]]
+    moves.append(
+        [
+            (total.at[:, pl.ds(at, hc)], to)
+            for at, to in ((plan.k_at, gk), (plan.v_at, gv), (plan.q_at, gq), (plan.o_at, go))
+        ]
+    )
+    moves.append(
+        [
+            (total.at[:, pl.ds(plan.gu_at + (2 * t + n) * LANES, LANES)], to.at[:, pl.ds(t * LANES, LANES)])
+            for t in range(ff // LANES)
+            for n, to in enumerate((gg, gu))
+        ]
+    )
+    moves.append([(total.at[:, pl.ds(plan.d_at, ff)], gd)])
+    stores = []
+    for load in loads:
+        load.start()
+    for load, group in zip(loads, moves):
         load.wait()
-        store.start()
-    gd[...] = total[:, plan.d_at : plan.d_at + ff]
-    for t in range(ff // LANES):
-        at = plan.gu_at + 2 * t * LANES
-        gg[:, t * LANES : (t + 1) * LANES] = total[:, at : at + LANES]
-        gu[:, t * LANES : (t + 1) * LANES] = total[:, at + LANES : at + 2 * LANES]
+        for src, to in group:
+            stores.append(pltpu.make_async_copy(src, to, store_sem.at[len(stores)]))
+            stores[-1].start()
     gains = jnp.transpose(total[:, 0:LANES])
     for i, ref in enumerate((g0, g1, g2, g3)):
         ref[...] = gains[i : i + 1, :]
@@ -1433,12 +1458,15 @@
             grad(sr, ff),
         )
         + (grad(1, sr),) * 4,
-        in_specs=[anywhere, anywhere, in_vmem],
-        out_specs=(anywhere, anywhere) + (in_vmem,) * 11,
+        in_specs=[anywhere] * 3,
+        out_specs=(anywhere,) * 9 + (in_vmem,) * 4,
         scratch_shapes=[
-            pltpu.VMEM((rows, width), bf16),
-            pltpu.VMEM((rows, width), f32),
-            pltpu.SemaphoreType.DMA((4,)),
+            (
+                pltpu.VMEM((rows, width), bf16),
+                pltpu.VMEM((rows, width), f32),
+                pltpu.VMEM((sr, plan.cols), f32),
+            ),
+            (pltpu.SemaphoreType.DMA((5,)), pltpu.SemaphoreType.DMA((7 + 2 * (ff // LANES),))),
         ],
         name="finish_layer",
     )(out, input_grad, total)

time: 310 us -> 303 us (0.977)
  Pallas kernels: 308 us -> 301 us
    pallas_call x1, Pallas kernels: 302 us -> 296 us  [fused_on_device(): pl.pallas_call(functools.partial(fused_layer, plan), out_shape=(jax.Shape...]
where the time goes in v3:
time: 303 us
  Pallas kernels  301 us (99%)
    pallas_call x1, Pallas kernels, fused_on_device(): pl.pallas_call(functools.partial(fused_layer, plan), out_shape=(jax.Shape...  296 us

profile of v3, /device:TPU:0, one launch (start us, length us, event | category | flops | bytes accessed | tf_op | source)
XLA Modules:
  0.0 302.8 jit_solution(12931184760822886532)
XLA Ops:
  0.6 1.3 maximum_convert_fusion.gain_shard
  1.9 296.1 %fused_layer.1 = (bf16[512,1024]{1,0:T(8,128)(2,1)}, f32[512,1024]{1,0:T(8,128)}, f32[64,6400]{1,0:T(8,128)}) custom-call(bf16[64,512]{1,0:T(8,128)(2,1)} %k_hbm.1, bf16[64,512]{1,0:T(8,128)(2,1)} %v_hbm.1, bf16[64,512]{1,0:T(8,128)(2,1)} %q_hbm.1, bf16[64,1408]{1,0:T(8,128)(2,1)} %g_hbm.1, bf16[64,1408]{1,0:T(8,128)(2,1)} %u_hbm.1, ...), custom_call_target="tpu_custom_call" | custom-call | tf_op jit(solution)/shard_map/fused_layer/pallas_call | solution.py:1425
  298.0 4.6 %finish_layer.1 = (bf16[512,1024]{1,0:T(8,128)(2,1)}, f32[512,1024]{1,0:T(8,128)}, f32[64,512]{1,0:T(8,128)}, f32[64,512]{1,0:T(8,128)}, f32[64,512]{1,0:T(8,128...) custom-call(bf16[512,1024]{1,0:T(8,128)(2,1)} %get-tuple-element.29., ...), custom_call_target="tpu_custom_call" | custom-call | tf_op jit(solution)/shard_map/finish_layer/pallas_call | solution.py:1447

commit v4 on v3

--- a/solution.py
+++ b/solution.py
@@ -383,7 +383,7 @@
 LATE_SLOTS = (0, 1, 6, 7, 8)
 X_FIRST = (1, 2)
 X_FIRST_SUM = (2, 2, 2, 2, 2, 2, 2, 2, 1, 1, 1, 1, 1, 1, 1, 1, 1, 1, 1, 1)
-PACE = (1, 2, 3, 4, 5, 6, 7, 8, 9, 10, 11, 12, 13)
+PACE = (1, 2, 3, 4, 5, 6, 7, 8, 9, 10, 11, 11, 12)
 TOKEN_PIECES = 8
 TOKENS_EARLY = 4
 TOKENS_A_STEP = 1
@@ -1061,15 +1061,18 @@
     events = sorted(
         ((j, phase) for j in range(n_reduce) for phase in range(5)), key=lambda e: (slot_of(*e), -e[0], e[1])
     )
-    done = [0]
+    pending = list(events)
 
     def pump(ready, until):
-        while done[0] < len(events):
-            j, phase = events[done[0]]
-            if j >= ready or slot_of(j, phase) >= until:
+        blocked = set()
+        for j, phase in list(pending):
+            if slot_of(j, phase) >= until:
                 break
-            rs_event(j, phase)
-            done[0] += 1
+            if j >= ready or j in blocked:
+                blocked.add(j)
+            else:
+                rs_event(j, phase)
+                pending.remove((j, phase))
 
     def back_tile(yy, t, bh):
         off = pl.multiple_of(t * 256, 256)

time: 303 us -> 299 us (0.987)
  Pallas kernels: 301 us -> 297 us
    pallas_call x1, Pallas kernels: 296 us -> 293 us  [fused_on_device(): pl.pallas_call(functools.partial(fused_layer, plan), out_shape=(jax.Shape...]
where the time goes in v4:
time: 299 us
  Pallas kernels  297 us (99%)
    pallas_call x1, Pallas kernels, fused_on_device(): pl.pallas_call(functools.partial(fused_layer, plan), out_shape=(jax.Shape...  293 us

profile of v4, /device:TPU:0, one launch (start us, length us, event | category | flops | bytes accessed | tf_op | source)
XLA Modules:
  0.0 299.3 jit_solution(17532947050089182167)
XLA Ops:
  0.6 1.3 maximum_convert_fusion.gain_shard
  1.9 292.6 %fused_layer.1 = (bf16[512,1024]{1,0:T(8,128)(2,1)}, f32[512,1024]{1,0:T(8,128)}, f32[64,6400]{1,0:T(8,128)}) custom-call(bf16[64,512]{1,0:T(8,128)(2,1)} %k_hbm.1, bf16[64,512]{1,0:T(8,128)(2,1)} %v_hbm.1, bf16[64,512]{1,0:T(8,128)(2,1)} %q_hbm.1, bf16[64,1408]{1,0:T(8,128)(2,1)} %g_hbm.1, bf16[64,1408]{1,0:T(8,128)(2,1)} %u_hbm.1, ...), custom_call_target="tpu_custom_call" | custom-call | tf_op jit(solution)/shard_map/fused_layer/pallas_call | solution.py:1428
  294.5 4.6 %finish_layer.1 = (bf16[512,1024]{1,0:T(8,128)(2,1)}, f32[512,1024]{1,0:T(8,128)}, f32[64,512]{1,0:T(8,128)}, f32[64,512]{1,0:T(8,128)}, f32[64,512]{1,0:T(8,128...) custom-call(bf16[512,1024]{1,0:T(8,128)(2,1)} %get-tuple-element.29., ...), custom_call_target="tpu_custom_call" | custom-call | tf_op jit(solution)/shard_map/finish_layer/pallas_call | solution.py:1450

commit v5 on v4

--- a/solution.py
+++ b/solution.py
@@ -383,7 +383,7 @@
 LATE_SLOTS = (0, 1, 6, 7, 8)
 X_FIRST = (1, 2)
 X_FIRST_SUM = (2, 2, 2, 2, 2, 2, 2, 2, 1, 1, 1, 1, 1, 1, 1, 1, 1, 1, 1, 1)
-PACE = (1, 2, 3, 4, 5, 6, 7, 8, 9, 10, 11, 11, 12)
+PACE = (1, 2, 3, 4, 5, 6, 7, 8, 9, 10, 11, 11, 11)
 TOKEN_PIECES = 8
 TOKENS_EARLY = 4
 TOKENS_A_STEP = 1

time: 299 us -> 309 us (1.033)
  Pallas kernels: 297 us -> 307 us
    pallas_call x1, Pallas kernels: 293 us -> 302 us  [fused_on_device(): pl.pallas_call(functools.partial(fused_layer, plan), out_shape=(jax.Shape...]
where the time goes in v5:
time: 309 us
  Pallas kernels  307 us (99%)
    pallas_call x1, Pallas kernels, fused_on_device(): pl.pallas_call(functools.partial(fused_layer, plan), out_shape=(jax.Shape...  302 us

profile of v5, /device:TPU:0, one launch (start us, length us, event | category | flops | bytes accessed | tf_op | source)
XLA Modules:
  0.0 309.1 jit_solution(17404058699231007911)
XLA Ops:
  0.6 1.3 maximum_convert_fusion.gain_shard
  1.9 302.3 %fused_layer.1 = (bf16[512,1024]{1,0:T(8,128)(2,1)}, f32[512,1024]{1,0:T(8,128)}, f32[64,6400]{1,0:T(8,128)}) custom-call(bf16[64,512]{1,0:T(8,128)(2,1)} %k_hbm.1, bf16[64,512]{1,0:T(8,128)(2,1)} %v_hbm.1, bf16[64,512]{1,0:T(8,128)(2,1)} %q_hbm.1, bf16[64,1408]{1,0:T(8,128)(2,1)} %g_hbm.1, bf16[64,1408]{1,0:T(8,128)(2,1)} %u_hbm.1, ...), custom_call_target="tpu_custom_call" | custom-call | tf_op jit(solution)/shard_map/fused_layer/pallas_call | solution.py:1428
  304.3 4.6 %finish_layer.1 = (bf16[512,1024]{1,0:T(8,128)(2,1)}, f32[512,1024]{1,0:T(8,128)}, f32[64,512]{1,0:T(8,128)}, f32[64,512]{1,0:T(8,128)}, f32[64,512]{1,0:T(8,128...) custom-call(bf16[512,1024]{1,0:T(8,128)(2,1)} %get-tuple-element.29., ...), custom_call_target="tpu_custom_call" | custom-call | tf_op jit(solution)/shard_map/finish_layer/pallas_call | solution.py:1450

commit v6 on v5

--- a/solution.py
+++ b/solution.py
@@ -379,11 +379,11 @@
 REDUCE_LAST = (256, 256)
 GATHER_LATE = 2
 LATE_STEP = 0
-REDUCE_LATE = 0
+REDUCE_LATE = 1
 LATE_SLOTS = (0, 1, 6, 7, 8)
 X_FIRST = (1, 2)
 X_FIRST_SUM = (2, 2, 2, 2, 2, 2, 2, 2, 1, 1, 1, 1, 1, 1, 1, 1, 1, 1, 1, 1)
-PACE = (1, 2, 3, 4, 5, 6, 7, 8, 9, 10, 11, 11, 11)
+PACE = (1, 2, 3, 4, 5, 6, 7, 8, 9, 10, 11, 12, 13)
 TOKEN_PIECES = 8
 TOKENS_EARLY = 4
 TOKENS_A_STEP = 1

time: 309 us -> 299 us (0.968)
  Pallas kernels: 307 us -> 297 us
    pallas_call x1, Pallas kernels: 302 us -> 292 us  [fused_on_device(): pl.pallas_call(functools.partial(fused_layer, plan), out_shape=(jax.Shape...]
where the time goes in v6:
time: 299 us
  Pallas kernels  297 us (99%)
    pallas_call x1, Pallas kernels, fused_on_device(): pl.pallas_call(functools.partial(fused_layer, plan), out_shape=(jax.Shape...  292 us

profile of v6, /device:TPU:0, one launch (start us, length us, event | category | flops | bytes accessed | tf_op | source)
XLA Modules:
  0.0 299.1 jit_solution(674124482508171488)
XLA Ops:
  0.6 1.3 maximum_convert_fusion.gain_shard
  1.9 292.4 %fused_layer.1 = (bf16[512,1024]{1,0:T(8,128)(2,1)}, f32[512,1024]{1,0:T(8,128)}, f32[64,6400]{1,0:T(8,128)}) custom-call(bf16[64,512]{1,0:T(8,128)(2,1)} %k_hbm.1, bf16[64,512]{1,0:T(8,128)(2,1)} %v_hbm.1, bf16[64,512]{1,0:T(8,128)(2,1)} %q_hbm.1, bf16[64,1408]{1,0:T(8,128)(2,1)} %g_hbm.1, bf16[64,1408]{1,0:T(8,128)(2,1)} %u_hbm.1, ...), custom_call_target="tpu_custom_call" | custom-call | tf_op jit(solution)/shard_map/fused_layer/pallas_call | solution.py:1428
  294.3 4.6 %finish_layer.1 = (bf16[512,1024]{1,0:T(8,128)(2,1)}, f32[512,1024]{1,0:T(8,128)}, f32[64,512]{1,0:T(8,128)}, f32[64,512]{1,0:T(8,128)}, f32[64,512]{1,0:T(8,128...) custom-call(bf16[512,1024]{1,0:T(8,128)(2,1)} %get-tuple-element.29., ...), custom_call_target="tpu_custom_call" | custom-call | tf_op jit(solution)/shard_map/finish_layer/pallas_call | solution.py:1450
